TPU v7x, 32 devices: a whole 2x2x4 slice. The times are simulated.
32 devices in a mesh: fsdp: 2 (over y), ctx: 4 (over z), tp: 4 (over x, core).
Axes of the slice: x: 2, y: 2, z: 4, core: 2. Of those that a mesh axis runs over, the one named last changes fastest.
Arguments:
- tokens: bfloat16 [5120, 2, 1024], P(('ctx', 'tp'), 'fsdp'), may hold values from -6 to 6
- first_values: bfloat16 [5120, 2, 1024], P('ctx', 'fsdp', 'tp'), may hold values from -6 to 6
- cotangent: bfloat16 [5120, 2, 1024], P(('ctx', 'tp'), 'fsdp'), may hold values from -6 to 6
- parents: int32 [2, 13], P('fsdp'), may hold values from 0 to 11, as said below
- seg_lengths: int32 [2, 13], P('fsdp'), may hold values from 1 to 2048, 5120 in all within a row
- w_query: bfloat16 [1024, 1024], P('fsdp', 'tp'), may hold values from -0.1875 to 0.1875
- w_key: bfloat16 [1024, 1024], P('fsdp', 'tp'), may hold values from -0.1875 to 0.1875
- w_value: bfloat16 [1024, 1024], P('fsdp', 'tp'), may hold values from -0.1875 to 0.1875
- w_out: bfloat16 [1024, 1024], P('fsdp', 'tp'), may hold values from -1.5 to 1.5
- w_gate: bfloat16 [1024, 2816], P('fsdp', 'tp'), may hold values from -0.1875 to 0.1875
- w_up: bfloat16 [1024, 2816], P('fsdp', 'tp'), may hold values from -0.1875 to 0.1875
- w_down: bfloat16 [1024, 2816], P('fsdp', 'tp'), may hold values from -0.109375 to 0.109375
- gain_attn: bfloat16 [1024], P('fsdp'), may hold values from 0.5 to 1.5
- gain_ffn: bfloat16 [1024], P('fsdp'), may hold values from 0.5 to 1.5
Outputs:
- layer_out: bfloat16 [5120, 2, 1024], P(('ctx', 'tp'), 'fsdp')
- grad_tokens: float32 [5120, 2, 1024], P(('ctx', 'tp'), 'fsdp')
- grad_values: float32 [5120, 2, 1024], P('ctx', 'fsdp', 'tp')
- grad_query: float32 [1024, 1024], P('fsdp', 'tp')
- grad_key: float32 [1024, 1024], P('fsdp', 'tp')
- grad_value: float32 [1024, 1024], P('fsdp', 'tp')
- grad_out: float32 [1024, 1024], P('fsdp', 'tp')
- grad_gate: float32 [1024, 2816], P('fsdp', 'tp')
- grad_up: float32 [1024, 2816], P('fsdp', 'tp')
- grad_down: float32 [1024, 2816], P('fsdp', 'tp')
- grad_gain_attn: float32 [1024], P('fsdp')
- grad_gain_ffn: float32 [1024], P('fsdp')
Inputs may be any that keep to these rules, and one draw needn't show every extreme that they name: `parents`: segment 0 of each tree is its root and names itself; every other segment's parent comes before it, at most 4 places back; the last segment's parent is the one just before it.
All inputs are finite; a program needn't handle non-finite values.
Results may differ from a plain program's by a relative error of at most 0.022.
Values may be sent and summed in bfloat16 or wider, within the bound.
No kernel may reach another device: no remote copies, remote signals or barrier semaphores. Data moves between devices by JAX's collectives and lax.ppermute only.
A program may use at most 192 MiB of HBM per device.

v0:
```python
import functools
import math

import jax
import jax.numpy as jnp
from jax import lax
from jax.experimental import pallas as pl
from jax.experimental.pallas import tpu as pltpu
from jax.sharding import PartitionSpec as P

HEAD = 64
HALF = HEAD // 2
BIG = 1e30
LOG2E = 1.4426950408889634
SCORE_SCALE = HEAD**-0.5
QUERY_SCALE = SCORE_SCALE * LOG2E
epsilon = 1e-05
f32 = jnp.float32
bf16 = jnp.bfloat16


def dot(a, b, ca, cb):
    return lax.dot_general(a, b, (((ca,), (cb,)), ((), ())), preferred_element_type=f32)


def layout_kernel(par_ref, len_ref, pos_ref, qx_ref, kx_ref, seg_ref, need_ref, anc_sc, above_sc, *, segs, tokens, piece):
    token = lax.broadcasted_iota(jnp.int32, (1, tokens), 1)
    pos = jnp.zeros((1, tokens), jnp.int32)
    seg_of = jnp.full((1, tokens), -1, jnp.int32)
    bits = jnp.zeros((1, tokens), jnp.int32)
    for b in range(tokens // piece):
        seg_ref[b] = 0
        need_ref[b] = 0
    off = jnp.int32(0)
    for s in range(segs):
        length = len_ref[0, s]
        if s == 0:
            anc, above = jnp.int32(1), jnp.int32(0)
        else:
            parent = par_ref[0, s]
            anc = anc_sc[parent] | jnp.int32(1 << s)
            above = above_sc[parent] + len_ref[0, parent]
        anc_sc[s] = anc
        above_sc[s] = above
        started = token >= off
        seg_of = jnp.where(started, s, seg_of)
        pos = jnp.where(started, token - off + above, pos)
        bits = jnp.where(started, anc, bits)

        def mark(b, carry, anc=anc, s=s):
            seg_ref[b] = seg_ref[b] | jnp.int32(1 << s)
            need_ref[b] = need_ref[b] | anc
            return carry

        lax.fori_loop(off // piece, (off + length - 1) // piece + 1, mark, 0)
        off = off + length
    row = lax.broadcasted_iota(jnp.int32, (kx_ref.shape[1], tokens), 0)
    key_extra = jnp.where(row == seg_of, -BIG, 0.0).astype(bf16)
    linked = lax.shift_right_logical(jnp.broadcast_to(bits, row.shape), row) & 1
    query_extra = jnp.where(linked == 1, 0.0, 1.0).astype(bf16)
    for p in range(tokens // piece):
        lanes = slice(p * piece, (p + 1) * piece)
        pos_ref[p] = pos[:, lanes].astype(f32)
        kx_ref[p] = key_extra[:, lanes]
        qx_ref[p] = query_extra[:, lanes]


SMEM = pl.BlockSpec(memory_space=pltpu.SMEM)
VMEM = pl.BlockSpec(memory_space=pltpu.VMEM)


def layout_call(parents, lengths, tokens, piece):
    segs = parents.shape[-1]
    rows = -(-segs // 16) * 16
    return pl.pallas_call(
        functools.partial(layout_kernel, segs=segs, tokens=tokens, piece=piece),
        out_shape=(
            jax.ShapeDtypeStruct((tokens // piece, 1, piece), f32),
            jax.ShapeDtypeStruct((tokens // piece, rows, piece), bf16),
            jax.ShapeDtypeStruct((tokens // piece, rows, piece), bf16),
            jax.ShapeDtypeStruct((tokens // piece,), jnp.int32),
            jax.ShapeDtypeStruct((tokens // piece,), jnp.int32),
        ),
        in_specs=[SMEM, SMEM],
        out_specs=(VMEM, VMEM, VMEM, SMEM, SMEM),
        scratch_shapes=[pltpu.SMEM((segs,), jnp.int32), pltpu.SMEM((segs,), jnp.int32)],
        cost_estimate=pl.CostEstimate(flops=0, bytes_accessed=1 << 16, transcendentals=0),
        name="layout",
    )(parents, lengths)


def causal(scores):
    key_at = lax.broadcasted_iota(jnp.int32, scores.shape, 0)
    query_at = lax.broadcasted_iota(jnp.int32, scores.shape, 1)
    return jnp.where(key_at <= query_at, scores, -BIG)


def three_parts(row):
    at = lax.broadcasted_iota(jnp.int32, (16, row.shape[1]), 0)
    high = row.astype(bf16).astype(f32)
    rest = row - high
    mid = rest.astype(bf16).astype(f32)
    low = rest - mid
    return jnp.where(at == 0, high, jnp.where(at == 1, mid, jnp.where(at == 2, low, 0.0))).astype(bf16)


def unrotate(values, cosine, sine):
    a, b = values[:HALF], values[HALF:]
    return jnp.concatenate([a * cosine + b * sine, b * cosine - a * sine], axis=0)


def prep_kernel(place_ref, qx_ref, kx_ref, got_ref, keys, key_lanes, value_lanes, values, queries):
    piece = got_ref.shape[2] // 2
    extra = qx_ref.shape[1]
    minus = jnp.full((16, piece), -1.0, bf16)
    pad_key = jnp.zeros((128 - HEAD - extra - 16, piece), bf16)
    pad_value = jnp.zeros((128 - HEAD - 16, piece), bf16)
    for half in (0, 1):
        for p in range(got_ref.shape[0]):
            at = 2 * p + (place_ref[0] ^ half)
            got = got_ref[p, :, half * piece : (half + 1) * piece]
            query, key, value = got[:HEAD, :], got[HEAD : 2 * HEAD, :], got[2 * HEAD :, :]
            key_lanes[at] = key
            keys[at] = jnp.concatenate([key, kx_ref[at], minus, pad_key], axis=0).T
            value_lanes[at] = jnp.concatenate([value, -minus], axis=0)
            values[at] = jnp.concatenate([value, minus, pad_value], axis=0).T
            queries[at] = jnp.concatenate([query, qx_ref[at], jnp.zeros((128 - HEAD - extra, piece), bf16)], axis=0)


def shape_of(*sizes, dtype=bf16):
    return jax.ShapeDtypeStruct(sizes, dtype)


def call(kernel, name, out_shape, operands, scratch=(), scalars=1, mib=20, late=()):
    outs = out_shape if isinstance(out_shape, tuple) else (out_shape,)
    arrays = operands[scalars:]
    count, total = len(arrays), len(arrays) + len(outs)

    def body(*refs):
        first, rest = refs[:scalars], refs[scalars:]
        outside, inside, sems, rest = rest[:total], rest[total : 2 * total], rest[2 * total], rest[2 * total + 1 :]
        copies = [pltpu.make_async_copy(outside[i], inside[i], sems.at[i]) for i in range(count)]
        for copy in copies:
            copy.start()
        for i in range(count):
            if i not in late:
                copies[i].wait()
        more = {"ready": lambda: [copies[i].wait() for i in late]} if late else {}
        kernel(*first, *inside, *rest, **more)
        copies = [pltpu.make_async_copy(inside[i], outside[i], sems.at[i]) for i in range(count, total)]
        for copy in copies:
            copy.start()
        for copy in copies:
            copy.wait()

    got = pl.pallas_call(
        body,
        out_shape=outs,
        in_specs=[SMEM] * scalars + [pl.BlockSpec(memory_space=pltpu.HBM)] * count,
        out_specs=(pl.BlockSpec(memory_space=pltpu.HBM),) * len(outs),
        scratch_shapes=[pltpu.VMEM(x.shape, x.dtype) for x in (*arrays, *outs)]
        + [pltpu.SemaphoreType.DMA((total,))]
        + list(scratch),
        compiler_params=pltpu.CompilerParams(vmem_limit_bytes=60 << 20),
        cost_estimate=pl.CostEstimate(flops=0, bytes_accessed=1 << 16, transcendentals=0),
        name=name,
    )(*operands)
    return got if isinstance(out_shape, tuple) else got[0]


def cut(ref, count):
    size = ref.shape[1] // count
    return [ref[:, i * size : (i + 1) * size] for i in range(count)]


def project_kernel(place_ref, near_own, near_other, far_own, far_other, gain_ref, cos_ref, sin_ref, first_ref, *rest, count, swap):
    weights, (out, near_out, far_out, raw) = rest[:count], rest[count:]
    heads_width = raw.shape[0] // 3
    size, width = near_own.shape
    block = width // count
    for refs, normed in (((near_own, near_other), near_out), ((far_own, far_other), far_out)):
        for half, ref in enumerate(refs):
            single = ref[...].astype(f32)
            scale = lax.rsqrt(jnp.mean(single * single, axis=-1, keepdims=True) + epsilon)
            if swap:
                turned = jnp.concatenate([single[:, block:], single[:, :block]], axis=1)
                single = jnp.where(place_ref[3] == 0, single, turned)
            at = pl.multiple_of((place_ref[1] ^ half) * size, size)
            normed[pl.ds(at, size), :] = (single * scale * gain_ref[...]).astype(bf16)
    piece = 2 * size
    turned = [[w[i * block : (i + 1) * block, :].T for w in weights] for i in range(3)]
    for half, rows_ref in enumerate((near_out, far_out)):
        rows = cut(rows_ref, count)
        for i in range(3):
            raw[i * heads_width : (i + 1) * heads_width, :] = sum(dot(w, r, 1, 1) for w, r in zip(turned[i], rows))
        x_half = place_ref[0] ^ half
        at = 2 * place_ref[2] + x_half
        cosine, sine = cos_ref[at], sin_ref[at]
        start = pl.multiple_of(x_half * piece, piece)
        first = first_ref[pl.ds(start, piece), :].astype(f32).T

        def turn(values):
            a, b = values[:HALF], values[HALF:]
            return jnp.concatenate([a * cosine - b * sine, b * cosine + a * sine], axis=0)

        lanes = slice(half * piece, (half + 1) * piece)
        for at in range(heads_width // HEAD):
            rows_at = [slice(i * heads_width + at * HEAD, i * heads_width + (at + 1) * HEAD) for i in range(3)]
            value = 0.5 * raw[rows_at[2], :] + 0.5 * first[at * HEAD : (at + 1) * HEAD]
            out[at, :HEAD, lanes] = (turn(raw[rows_at[0], :]) * QUERY_SCALE).astype(bf16)
            out[at, HEAD : 2 * HEAD, lanes] = turn(raw[rows_at[1], :]).astype(bf16)
            out[at, 2 * HEAD :, lanes] = value.astype(bf16)


def project_call(place, rows, gain, cosine, sine, first, weights, swap):
    (size, width), columns = rows[0].shape, weights[0].shape[1]
    return call(
        functools.partial(project_kernel, count=len(weights), swap=swap), "project",
        (shape_of(columns // HEAD, 3 * HEAD, 4 * size), shape_of(2 * size, width), shape_of(2 * size, width)),
        (place, *rows, gain, cosine, sine, first, *weights),
        scratch=[pltpu.VMEM((3 * columns, 2 * size), f32)],
    )


def stack_kernel(*refs):
    out, at = refs[-1], 0
    for ref in refs[:-1]:
        rows = ref.shape[0]
        out[at : at + rows, :] = ref[...]
        at += rows


def pick_kernel(*refs):
    out = refs[-1]
    rows = out.shape[0]
    size = out.shape[1] // (len(refs) - 1)
    for i, ref in enumerate(refs[:-1]):
        out[:, i * size : (i + 1) * size] = ref[ref.shape[0] - rows :, :]


def pick_call(blocks, rows):
    return call(pick_kernel, "pick", shape_of(rows, blocks[0].shape[1] * len(blocks)), tuple(blocks), scalars=0)


def stack_call(*arrays):
    rows = sum(a.shape[0] for a in arrays)
    return call(stack_kernel, "stack", shape_of(rows, arrays[0].shape[1]), arrays, scalars=0, mib=16)


def split_core(place_ref, total, mine_ref, other_ref):
    rows = mine_ref.shape[0]
    mine_ref[...] = total[pl.ds(pl.multiple_of(place_ref[1] * rows, rows), rows), :]
    other_ref[...] = total[pl.ds(pl.multiple_of((1 - place_ref[1]) * rows, rows), rows), :].astype(bf16)


def output_kernel(place_ref, near_ref, far_ref, *rest):
    near_weight, far_weight, mine_ref, other_ref, total = rest
    total[...] = dot(near_ref[...].T, near_weight[...], 1, 0) + dot(far_ref[...].T, far_weight[...], 1, 0)
    split_core(place_ref, total, mine_ref, other_ref)


def output_call(place, near, far, near_weight, far_weight):
    rows, width = near.shape[1], near_weight.shape[1]
    return call(
        output_kernel, "out_project",
        (shape_of(rows // 2, width, dtype=f32), shape_of(rows // 2, width)),
        (place, near, far, near_weight, far_weight),
        scratch=[pltpu.VMEM((rows, width), f32)],
    )


def heads_kernel(place_ref, own_ref, other_ref, near_weight, far_weight, near_out, far_out, chip):
    rows = own_ref.shape[0]
    for half, ref in enumerate((own_ref, other_ref)):
        chip[pl.ds(pl.multiple_of((place_ref[1] ^ half) * rows, rows), rows), :] = ref[...]
    far_out[...] = dot(far_weight[...], chip[...], 1, 1).astype(bf16)
    near_out[...] = dot(near_weight[...], chip[...], 1, 1).astype(bf16)


def heads_call(place, own, other, near_weight, far_weight):
    rows, columns = 2 * own.shape[0], near_weight.shape[0]
    return call(
        heads_kernel, "out_back",
        (shape_of(columns, rows), shape_of(columns, rows), shape_of(rows, own.shape[1])),
        (place, own, other, near_weight, far_weight),
    )


def feed_kernel(rows_ref, other_ref, cot_ref, cot_other_ref, *rest, count):
    hidden = rest[count].shape[2]
    gate_w, up_w, down_w = ([w.at[i * hidden : (i + 1) * hidden] for w in rest[:count]] for i in range(3))
    hidden_ref, gate_ref, up_ref, mine_ref, sent_ref, rows_sc, cot_sc, back_sc = rest[count:]
    size = rows_ref.shape[0]
    rows_sc[0], rows_sc[1] = rows_ref[...], other_ref[...]
    cot_sc[0], cot_sc[1] = cot_ref[...], cot_other_ref[...]
    block = rows_ref.shape[1] // count

    def step(at, carry):
        lanes = [slice(i * block, (i + 1) * block) for i in range(count)]
        rows, cots = [rows_sc[at, :, s] for s in lanes], [cot_sc[at, :, s] for s in lanes]
        gate = sum(dot(r, w[...], 1, 1) for r, w in zip(rows, gate_w))
        up = sum(dot(r, w[...], 1, 1) for r, w in zip(rows, up_w))
        hidden_grad = sum(dot(r, w[...], 1, 1) for r, w in zip(cots, down_w))
        sig = 1.0 / (1.0 + jnp.exp(-gate))
        act = gate * sig
        hidden_ref[at] = (act * up).astype(bf16)
        gate_grad = (hidden_grad * up * (sig * (1.0 + gate * (1.0 - sig)))).astype(bf16)
        up_grad = (hidden_grad * act).astype(bf16)
        gate_ref[at] = gate_grad
        up_ref[at] = up_grad
        for i in range(count):
            back_sc[at, :, lanes[i]] = dot(gate_grad, gate_w[i][...], 1, 0) + dot(up_grad, up_w[i][...], 1, 0)
        return carry

    lax.fori_loop(0, 2, step, 0)
    mine_ref[...] = back_sc[0]
    sent_ref[...] = back_sc[1].astype(bf16)


def feed_call(rows, other, cot, cot_other, weights, hidden):
    size, width = rows.shape
    count = len(weights)
    return call(
        functools.partial(feed_kernel, count=count), "feed",
        (shape_of(2, size, hidden),) * 3 + (shape_of(size, width, dtype=f32), shape_of(size, width)),
        (rows, other, cot, cot_other, *weights),
        scratch=[pltpu.VMEM((2, size, width), bf16)] * 2 + [pltpu.VMEM((2, size, width), f32)],
        scalars=0, mib=40,
    )


def prep_back(place_ref, queries, near_grad, far_grad, near_full, far_full, near_lse, far_lse, queries_out, grads_out, extra):
    places, _, piece = near_grad.shape
    queries_out[...] = queries[...]
    pad = jnp.zeros((128 - HEAD - 16, piece), bf16)
    for half, (grad, full, lse) in enumerate(((near_grad, near_full, near_lse), (far_grad, far_full, far_lse))):
        for p in range(places):
            at = 2 * p + (place_ref[0] ^ half)
            queries_out[at, HEAD + extra : HEAD + extra + 16, :] = lse[p]
            delta = jnp.sum(grad[p].astype(f32) * full[p], axis=0, keepdims=True)
            grads_out[at] = jnp.concatenate([grad[p], three_parts(delta), pad], axis=0)


def by_projection(kv, last):
    columns = kv.shape[0] * HEAD
    flat = lambda ref, at: ref[:, at * HEAD : (at + 1) * HEAD, :].reshape(columns, ref.shape[2])
    return (flat(last, 2), flat(last, 0), flat(last, 1)), (flat(last, 3), flat(kv, 0), flat(kv, 1))


def weights_kernel(near_rows, far_rows, kv, last, *parts):
    size = near_rows.shape[1] // len(parts)
    near, far = by_projection(kv, last)
    for i in range(3):
        for b, part in enumerate(parts):
            lanes = slice(b * size, (b + 1) * size)
            sums = dot(near[i], near_rows[:, lanes], 1, 0) + dot(far[i], far_rows[:, lanes], 1, 0)
            part[i * size : (i + 1) * size, :] = sums.T.astype(bf16)


def weights_call(near_rows, far_rows, kv, last, count):
    width, columns = near_rows.shape[1], kv.shape[0] * HEAD
    return call(
        weights_kernel, "weight_grads", tuple(shape_of(3 * width // count, columns) for _ in range(count)),
        (near_rows, far_rows, kv, last), scalars=0,
    )


def rows_kernel(place_ref, near_rows, far_rows, kv, last, *rest, count):
    weights, (near_mine, near_other, far_mine, far_other, gain_ref, value_ref, total) = rest[:count], rest[count:]
    size = near_rows.shape[1] // count
    near, far = by_projection(kv, last)
    for half, grads in enumerate((near, far)):
        value = grads[2].T.astype(f32)
        tokens, columns = value.shape
        folds = columns // 128
        for j in range(folds):
            rows_at = pl.ds((place_ref[0] ^ half) * tokens * folds + j, tokens, stride=folds)
            value_ref[rows_at, :] = value[:, j * 128 : (j + 1) * 128]
    gain_ref[...] = jnp.zeros(gain_ref.shape, f32)
    for grads, rows, mine, other in ((far, far_rows, far_mine, far_other), (near, near_rows, near_mine, near_other)):
        turned = [g.T for g in grads]
        for b in range(count):
            lanes = slice(b * size, (b + 1) * size)
            part = sum(dot(g, weights[b][i * size : (i + 1) * size, :], 1, 1) for i, g in enumerate(turned))
            total[:, lanes] = part
            gain_ref[:, lanes] += jnp.sum(part * rows[:, lanes].astype(f32), axis=0, keepdims=True)
        split_core(place_ref, total, mine, other)


def rows_call(place, near_rows, far_rows, kv, last, weights):
    size, width = near_rows.shape
    rows = (shape_of(size // 2, width, dtype=f32), shape_of(size // 2, width))
    values = shape_of(2 * size * kv.shape[0] * HEAD // 128, 128, dtype=f32)
    return call(
        functools.partial(rows_kernel, count=len(weights)), "rows_back",
        rows + rows + (shape_of(1, width, dtype=f32), values),
        (place, near_rows, far_rows, kv, last, *weights),
        scratch=[pltpu.VMEM((size, width), f32)],
    )


def feed_grads_kernel(near_gate, far_gate, near_up, far_up, near_hidden, far_hidden, *refs):
    rows, cots, outs = refs[:4], refs[4:8], refs[8:]
    count = len(outs) // 2
    size = rows[0].shape[1] // count
    hidden = near_gate.shape[2]
    pairs = ((near_gate, far_gate, rows), (near_up, far_up, rows), (near_hidden, far_hidden, cots))
    for b in range(count):
        lanes = slice(b * size, (b + 1) * size)
        for i, (near, far, right) in enumerate(pairs):
            near, far = (ref[...].reshape(2 * ref.shape[1], hidden) for ref in (near, far))
            near_right, far_right = (jnp.concatenate([right[j][:, lanes], right[j + 1][:, lanes]], axis=0) for j in (0, 2))
            total = (dot(near, near_right, 0, 0) + dot(far, far_right, 0, 0)).astype(bf16)
            if i < 2:
                outs[b][i * hidden : (i + 1) * hidden, :] = total
            else:
                outs[count + b][...] = total


def feed_grads_call(lefts, hiddens, rows, cots, count):
    hidden, size = lefts[0].shape[2], rows[0].shape[1] // count
    outs = call(
        feed_grads_kernel, "feed_grads",
        (shape_of(2 * hidden, size),) * count + (shape_of(hidden, size),) * count,
        (*lefts, *hiddens, *rows, *cots), scalars=0, mib=40,
    )
    return outs[:count], outs[count:]


def result_kernel(near_hidden, far_hidden, *rest, count):
    weights, (near_mine, far_mine, sent) = rest[:count], rest[count:]
    size = near_mine.shape[1] // count
    for at, (ref, mine) in enumerate(((near_hidden, near_mine), (far_hidden, far_mine))):
        for i in range(count):
            lanes = slice(i * size, (i + 1) * size)
            weight = weights[i][2 * ref.shape[2] : 3 * ref.shape[2], :]
            mine[:, lanes] = dot(ref[0], weight, 1, 0)
            sent[at, :, lanes] = dot(ref[1], weight, 1, 0).astype(bf16)


def result_call(near_hidden, far_hidden, weights):
    _, size, _ = near_hidden.shape
    count = len(weights)
    width = weights[0].shape[1] * count
    return call(
        functools.partial(result_kernel, count=count), "result",
        (shape_of(size, width, dtype=f32), shape_of(size, width, dtype=f32), shape_of(2, size, width)),
        (near_hidden, far_hidden, *weights), scalars=0, mib=24,
    )


def out_grads_kernel(place_ref, chip_low, far_own, far_other, near_mixed, far_mixed, *rest):
    outs, far_low = rest[:-1], rest[-1]
    count = len(outs)
    rows = far_own.shape[0]
    for half, ref in enumerate((far_own, far_other)):
        far_low[pl.ds(pl.multiple_of((place_ref[1] ^ half) * rows, rows), rows), :] = ref[...]
    near, far = near_mixed[...], far_mixed[...]
    for out, near_rows, far_rows in zip(outs, cut(chip_low, count), cut(far_low, count)):
        out[...] = (dot(near, near_rows, 1, 0) + dot(far, far_rows, 1, 0)).T.astype(bf16)


def out_grads_call(place, chip_low, far_own, far_other, near_mixed, far_mixed, count):
    width, columns = chip_low.shape[1] // count, near_mixed.shape[0]
    return call(
        out_grads_kernel, "out_grads", tuple(shape_of(width, columns) for _ in range(count)),
        (place, chip_low, far_own, far_other, near_mixed, far_mixed),
        scratch=[pltpu.VMEM(chip_low.shape, bf16)],
    )


def join_kernel(*refs):
    count = len(refs) // 3
    for i in range(count):
        a, b, out = refs[2 * i], refs[2 * i + 1], refs[2 * count + i]
        out[...] = (a[...].astype(f32) + b[...].astype(f32)).astype(bf16)


def join_call(*pairs):
    outs = call(
        join_kernel, "join", tuple(shape_of(*a.shape) for a, _ in pairs), [x for pair in pairs for x in pair],
        scalars=0, mib=16,
    )
    return list(outs)


def collect(first, last, hit, todo):
    def step(at, count):
        todo[count] = at
        return count + hit(at).astype(jnp.int32)

    return lax.fori_loop(first, last, step, jnp.int32(0))


def two_ahead(count, todo, first, fill, work):
    def step(j, now):
        middle, after = todo[2 * j], todo[2 * j + 1]
        fill(1, middle)
        work(0, now)
        fill(0, after)
        work(1, middle)
        return after

    last = lax.fori_loop(0, count // 2, step, first)

    @pl.when(lax.rem(count, 2) == 0)
    def _():
        work(0, last)

    @pl.when(lax.rem(count, 2) == 1)
    def _():
        final = todo[count - 1]
        fill(1, final)
        work(0, last)
        work(1, final)


def fwd_kernel(todo_ref, place_ref, seg_ref, need_ref, *refs, first):
    outs, (score_a, score_b, top, total, todo) = refs[:-5], refs[-5:]
    if first:
        got_ref, qx_ref, kx_ref, out_ref, full_ref, lse_ref, keys, key_lanes, values, plain_values, queries = outs
        prep_kernel(place_ref, qx_ref, kx_ref, got_ref, keys, key_lanes, values, plain_values, queries)
    else:
        keys, values, queries, out_ref, full_ref, lse_ref = outs
    scores = (score_a, score_b)

    def attend(i, carry):
        at = todo_ref[i]
        need = need_ref[at]
        count = collect(0, at, lambda k: (seg_ref[k] & need) != 0, todo)
        query = queries[at]
        score_a[...] = causal(dot(keys[at], query, 1, 0))
        top[...] = jnp.full(top.shape, -BIG, f32)
        total[...] = jnp.zeros(total.shape, f32)

        def fill(slot, key_at):
            scores[slot][...] = dot(keys[key_at], query, 1, 0)

        def work(slot, key_at):
            score = scores[slot][...]
            old_top = top[...]
            new_top = jnp.maximum(old_top, jnp.max(score, axis=0, keepdims=True))
            weights = jnp.exp2(score - new_top).astype(bf16)
            total[...] = total[...] * jnp.exp2(old_top - new_top) + dot(values[key_at], weights, 1, 0)
            top[...] = new_top

        two_ahead(count, todo, at, fill, work)
        final = total[...]
        weight_sum = final[HEAD : HEAD + 1, :]
        mixed = final[:HEAD, :] * (1.0 / weight_sum)
        out_ref[i] = mixed.astype(bf16)
        full_ref[i] = mixed
        lse_ref[i] = three_parts(top[...] + jnp.log2(weight_sum))
        return carry

    lax.fori_loop(0, out_ref.shape[0], attend, 0)


def fwd_call(todo, place, seg, need, operands, first=False):
    count = todo.shape[0]
    if first:
        pieces, piece = 2 * operands[0].shape[0], operands[0].shape[2] // 2
        more = (
            shape_of(pieces, piece, 128),
            shape_of(pieces, HEAD, piece),
            shape_of(pieces, HEAD + 16, piece),
            shape_of(pieces, piece, 128),
            shape_of(pieces, 128, piece),
        )
    else:
        (pieces, _, piece), more = operands[2].shape, ()
    return call(
        functools.partial(fwd_kernel, first=first), "attend",
        (shape_of(count, HEAD, piece), shape_of(count, HEAD, piece, dtype=f32), shape_of(count, 16, piece)) + more,
        (todo, place, seg, need, *operands),
        scratch=[pltpu.VMEM((piece, piece), f32)] * 2
        + [pltpu.VMEM((1, piece), f32), pltpu.VMEM((HEAD + 16, piece), f32), pltpu.SMEM((pieces,), jnp.int32)],
        scalars=4,
    )


def bwd_kernel(todo_ref, place_ref, seg_ref, need_ref, cos_ref, sin_ref, keys, key_lanes, values, queries, *rest, stage, todo_count, extra, ready):
    if stage:
        grads, kept, sum_in, rest = rest[0], rest[1], rest[2], rest[3:]
    else:
        before, rest = rest[:6], rest[6:]
    outs, rest = rest[: (4, 3, 1)[stage]], rest[(4, 3, 1)[stage] :]
    if not stage:
        prep_back(place_ref, queries, *before, outs[1], outs[2], extra)
        queries, grads = outs[1], outs[2]
    score_a, grad_a, score_b, grad_b, key_sum, value_sum, todo = rest[:7]
    sums = rest[7] if stage == 2 else outs[-1]
    pieces = queries.shape[0]
    scores, prob_grads = (score_a, score_b), (grad_a, grad_b)
    sums[...] = sum_in[...] if stage else jnp.zeros(sums.shape, f32)
    if stage == 1:
        outs[0][:2] = kept[...]
    if stage == 2:
        outs[0][2:, : 2 * HEAD, :] = kept[...]
    ready()

    def attend(i, carry):
        at = todo_ref[i]
        seg = seg_ref[at]
        count = collect(at + 1, pieces, lambda q: (need_ref[q] & seg) != 0, todo)
        key, value, key_lane = keys[at], values[at], key_lanes[at]
        score_a[...] = causal(dot(key, queries[at], 1, 0))
        grad_a[...] = dot(value, grads[at], 1, 0)
        key_sum[...] = jnp.zeros(key_sum.shape, f32)
        value_sum[...] = jnp.zeros(value_sum.shape, f32)

        def fill(slot, query_at):
            scores[slot][...] = dot(key, queries[query_at], 1, 0)
            prob_grads[slot][...] = dot(value, grads[query_at], 1, 0)

        def work(slot, query_at):
            probs = jnp.exp2(scores[slot][...])
            score_grad = (probs * prob_grads[slot][...]).astype(bf16)
            value_sum[...] += dot(grads[query_at, :HEAD, :], probs.astype(bf16), 1, 1)
            key_sum[...] += dot(queries[query_at, :HEAD, :], score_grad, 1, 1)
            sums[query_at] += dot(key_lane, score_grad, 1, 0)

        two_ahead(count, todo, at, fill, work)
        key_grad = unrotate(key_sum[...] * (1.0 / LOG2E), cos_ref[at], sin_ref[at]).astype(bf16)
        value_grad = (0.5 * value_sum[...]).astype(bf16)

        def write(ref, place):
            ref[place, :HEAD, :] = key_grad
            ref[place, HEAD : 2 * HEAD, :] = value_grad

        if stage == 1:
            pl.when(i < 2)(lambda: write(outs[0], 2 + i))
            pl.when(i >= 2)(lambda: write(outs[1], i - 2))
        else:
            write(outs[0], i)
        return carry

    lax.fori_loop(0, todo_count, attend, 0)
    if stage == 2:
        for p in range(pieces):
            grad = unrotate(sums[p] * SCORE_SCALE, cos_ref[p], sin_ref[p]).astype(bf16)
            start = pl.multiple_of((2 + ((p % 2) ^ place_ref[0])) * HEAD, HEAD)
            outs[0][p // 2, pl.ds(start, HEAD), :] = grad


def bwd_call(stage, todo, place, seg, need, cosine, sine, keys, key_lanes, values, queries, more, extra):
    count, (pieces, _, piece) = todo.shape[0], queries.shape
    places = pieces // 2
    sums = shape_of(pieces, HEAD, piece, dtype=f32)
    outs = (
        (shape_of(2, 2 * HEAD, piece), shape_of(*queries.shape), shape_of(*queries.shape), sums),
        (shape_of(places, 2 * HEAD, piece), shape_of(2, 2 * HEAD, piece), sums),
        (shape_of(places, 4 * HEAD, piece),),
    )[stage]
    operands = (cosine, sine, keys, key_lanes, values, queries, *more)
    got = call(
        functools.partial(bwd_kernel, stage=stage, todo_count=count, extra=extra), "attend_back", outs,
        (todo, place, seg, need, *operands),
        scratch=[pltpu.VMEM((piece, piece), f32)] * 4
        + [pltpu.VMEM((HEAD, piece), f32)] * 2
        + [pltpu.SMEM((pieces,), jnp.int32)]
        + ([pltpu.VMEM(sums.shape, f32)] if stage == 2 else []),
        scalars=4, mib=36, late=(0, 1),
    )
    return got[0] if stage == 2 else got


def after(value, *earlier):
    return lax.optimization_barrier((value,) + earlier)[0]


def on_device(
    tokens, first_values, cotangent, parents, seg_lengths,
    w_query, w_key, w_value, w_out, w_gate, w_up, w_down, gain_attn, gain_ffn,
):
    assert tokens.shape[1] == 1
    fsdp_count, ctx_count, tp_count = (lax.axis_size(a) for a in ("fsdp", "ctx", "tp"))
    assert tp_count == 4 and ctx_count == 4
    fsdp_at, ctx_at, tp_at = (lax.axis_index(a) for a in ("fsdp", "ctx", "tp"))
    core_at, x_at = tp_at % 2, tp_at // 2
    own_rows, width = tokens.shape[0], tokens.shape[2]
    chip_rows = 2 * own_rows
    heads = w_query.shape[1] // HEAD
    head_width = heads * HEAD
    assert heads == ctx_count
    tree_len = own_rows * tp_count * ctx_count
    weight_rows, hidden = w_query.shape[0], w_gate.shape[1]
    two = fsdp_count == 2

    def over_core(value):
        return lax.ppermute(value, "tp", [(i, i ^ 1) for i in range(tp_count)])

    def over_x(value):
        return lax.ppermute(value, "tp", [(i, i ^ 2) for i in range(tp_count)])

    def over_fsdp(value):
        return lax.ppermute(value, "fsdp", [(0, 1), (1, 0)])

    def over_ctx(value, flip):
        return lax.ppermute(value, "ctx", [(i, i ^ flip) for i in range(ctx_count)])

    def exchange(by_place):
        return lax.all_to_all(by_place, "ctx", 0, 0, tiled=True)

    def relative(rows):
        if not two:
            return rows
        swapped = jnp.concatenate([rows[..., weight_rows:], rows[..., :weight_rows]], axis=-1)
        return jnp.where(fsdp_at == 0, rows, swapped)

    def by_x(near, far):
        return jnp.where(x_at == 0, jnp.concatenate([near, far], axis=0), jnp.concatenate([far, near], axis=0))

    def fsdp_sum(parts, axis=0):
        if not two:
            return lax.psum_scatter(parts[0], "fsdp", scatter_dimension=axis, tiled=True)
        return parts[0], over_fsdp(parts[1])

    def inward(low):
        return low, lax.ppermute(low, "ctx", [(0, 1), (3, 2)])

    def across(low):
        return low, lax.ppermute(low, "ctx", [(1, 2), (2, 1)])

    def outward(low):
        return low, lax.ppermute(low, "ctx", [(1, 0), (2, 3)])

    def join(pair):
        return (pair[0].astype(f32) + pair[1].astype(f32)).astype(bf16)

    def finish(pair):
        return jnp.where((ctx_at == 0) | (ctx_at == 3), pair[1], pair[0]).astype(f32)

    def hold(pair, *earlier):
        return (pair[0], after(pair[1], *earlier)) if isinstance(pair, tuple) else after(pair, *earlier)

    def step(*pairs):
        if not two:
            return [join(pair) if isinstance(pair, tuple) else pair for pair in pairs]
        return join_call(*pairs)

    three = (w_query, w_key, w_value)
    own_tokens, early_gains = tokens[:, 0, :], jnp.stack([gain_attn, gain_ffn])
    if two:
        own_three = stack_call(*three)
        qkv_weight = [own_three, over_fsdp(own_three)]
        own_tokens, early_gains = after(own_tokens, own_three), after(early_gains, own_three)
        gains = jnp.concatenate([early_gains, over_fsdp(early_gains)], axis=1)
    else:
        qkv_weight = [stack_call(*(lax.all_gather(w, "fsdp", axis=0, tiled=True) for w in three))]
        gains = lax.all_gather(early_gains, "fsdp", axis=1, tiled=True)
    token_x = over_x(own_tokens)
    token_core = over_core(own_tokens)
    attention_gain = gains[0].reshape(1, width).astype(f32)
    ffn_gain = gains[1].reshape(1, width).astype(f32)
    count = len(qkv_weight)

    place = jnp.stack([x_at, core_at, ctx_at, fsdp_at]).astype(jnp.int32)
    position, query_extra, key_extra, seg_bits, need_bits = layout_call(parents, seg_lengths, tree_len, chip_rows)
    frequency = jnp.exp(-math.log(10000.0) * jnp.arange(HALF, dtype=f32) / HALF)
    angles = frequency[None, :, None] * position
    cosine, sine = jnp.cos(angles), jnp.sin(angles)

    def normalize(rows_f32):
        return lax.rsqrt(jnp.mean(rows_f32 * rows_f32, axis=-1, keepdims=True) + epsilon)

    first_flat = first_values[:, 0, :]

    def spread(pieces):
        return [over_ctx(piece, flip) if flip else piece for flip, piece in enumerate(pieces)]

    by_head, near_normed, far_normed = project_call(
        place, (own_tokens, token_core, token_x, over_core(token_x)), attention_gain, cosine, sine, first_flat, qkv_weight, two
    )
    got = exchange(by_head)
    others = (w_gate, w_up, w_down, w_out)
    if two:
        feed_own = stack_call(*(after(w.T, by_head) for w in others))
        feed_weight = [feed_own, over_fsdp(feed_own)]
    else:
        feed_weight = [stack_call(*(lax.all_gather(w, "fsdp", axis=0, tiled=True).T for w in others))]
    own_cot = relative(after(cotangent[:, 0, :], by_head))
    half_places = jnp.arange(ctx_count, dtype=jnp.int32) * 2
    far_out, far_full, far_lse, keys, key_lanes, value_lanes, values, queries = fwd_call(
        after(half_places + (1 - x_at), own_cot), place, seg_bits, need_bits, (got, query_extra, key_extra), True
    )
    cot_x = over_x(after(own_cot, got))
    out_weight = pick_call([after(w, far_out) for w in feed_weight], head_width)
    out_weight_x = over_x(out_weight)
    cot_core = over_core(after(own_cot, got))
    cot_x_core = over_core(cot_x)

    near_out, near_full, near_lse = fwd_call(
        after(half_places + x_at, far_out, out_weight, cot_x), place, seg_bits, need_bits, (keys, value_lanes, queries)
    )
    far_mixed = after(exchange(far_out), near_out).reshape(head_width, chip_rows)
    far_mixed_got = over_x(far_mixed)
    near_mixed = exchange(after(near_out, far_mixed)).reshape(head_width, chip_rows)

    mine, other = output_call(place, near_mixed, far_mixed_got, out_weight, out_weight_x)
    own_single = relative(own_tokens).astype(f32)
    middle = own_single + mine + over_core(other).astype(f32)

    middle_scale = normalize(middle)
    ffn_own = (middle * middle_scale * ffn_gain).astype(bf16)
    ffn_x = over_x(ffn_own)
    ffn_core = over_core(ffn_own)
    near_hidden, near_gate, near_up, near_mine, near_sent = feed_call(
        ffn_own, ffn_core, own_cot, cot_core, feed_weight, hidden
    )
    ffn_x = after(ffn_x, near_mine)
    ffn_x_core = over_core(ffn_x)
    far_hidden, far_gate, far_up, far_mine, far_sent = feed_call(
        ffn_x, ffn_x_core, cot_x, cot_x_core, feed_weight, hidden
    )
    far_sum = (far_mine + over_core(far_sent).astype(f32)).astype(bf16)
    far_sum_got = over_x(far_sum)
    near_sum = near_mine + over_core(near_sent).astype(f32)

    all_cot = (after(own_cot, far_sum), cot_core, cot_x, cot_x_core)
    all_ffn = (after(ffn_own, far_sum), ffn_core, ffn_x, ffn_x_core)
    first_parts, second_parts = feed_grads_call(
        (near_gate, far_gate, near_up, far_up), (near_hidden, far_hidden), all_ffn, all_cot, count
    )
    first_sum = fsdp_sum(first_parts, 1)
    second_sum = fsdp_sum(second_parts, 1)
    ffn_grad = near_sum + after(far_sum_got, first_parts[0]).astype(f32)

    weighted = ffn_grad * ffn_gain
    middle_grad = (
        own_cot.astype(f32)
        + middle_scale * weighted
        - middle * (middle_scale**3 * jnp.mean(weighted * middle, axis=-1, keepdims=True))
    )
    middle_low = middle_grad.astype(bf16)
    near_heads, far_heads, chip_low = heads_call(place, middle_low, over_core(middle_low), out_weight, out_weight_x)
    far_out_grad = over_x(far_heads)
    near_grads = exchange(near_heads.reshape(heads, HEAD, chip_rows))
    far_grads = exchange(after(far_out_grad, near_grads).reshape(heads, HEAD, chip_rows))

    ffn_gain_part = jnp.sum(after(ffn_grad, near_heads) * middle * middle_scale, axis=0)
    low_x = over_x(after(middle_low, far_out_grad))
    low_x_core = over_core(low_x)
    near_result, far_result, sent = result_call(after(near_hidden, near_heads), far_hidden, feed_weight)
    sent_got = over_core(sent)
    (first_low,) = step(hold(first_sum, far_grads, sent))
    first_in = inward(first_low)
    def back(stage, places, more, *earlier):
        return bwd_call(
            stage, after(jnp.stack(places).astype(jnp.int32), *earlier), place, seg_bits, need_bits, cosine, sine,
            keys, key_lanes, values, more[0], more[1:], query_extra.shape[1],
        )

    far_at, near_at = [2 * i + 1 - x_at for i in range(4)], [2 * i + x_at for i in range(4)]
    first_kv, back_queries, grads, query_sum = back(
        0, far_at[:2], (queries, near_grads, far_grads, near_full, far_full, near_lse, far_lse), first_low
    )

    first_low, second_low = step(hold(first_in, first_kv), hold(second_sum, first_kv))
    first_across, second_in = across(first_low), inward(second_low)
    far_kv, near_kv, query_sum = back(
        1, far_at[2:] + near_at[2:], (back_queries, grads, first_kv, query_sum), first_low
    )

    first_low, second_low = step(hold(first_across, far_kv), hold(second_in, far_kv))
    first_done, second_across = outward(first_low), across(second_low)
    far_kv_got = exchange(after(far_kv, first_low))
    last = back(2, near_at[:2], (back_queries, grads, near_kv, query_sum), first_low)

    (second_low,) = step(hold(second_across, last))
    second_done = outward(second_low)
    last_got = exchange(after(last, second_low, first_done[1]))
    far_kv_got = after(far_kv_got, last)
    out_parts = out_grads_call(after(place, last), chip_low, low_x, low_x_core, near_mixed, far_mixed, count)
    out_sum = fsdp_sum(out_parts)
    far_result_got = over_x((after(far_result, out_parts[0]) + sent_got[1].astype(f32)).astype(bf16))
    second_all = finish(hold(second_done, out_parts[0]))
    layer_out = relative((after(middle, second_all) + near_result + sent_got[0].astype(f32) + far_result_got.astype(f32)).astype(bf16))
    first_all = finish(hold(first_done, second_low))
    (out_low,) = step(hold(out_sum, layer_out))
    last_got = after(last_got, first_all, out_low)
    out_in = inward(out_low)

    qkv_parts = weights_call(near_normed, far_normed, far_kv_got, last_got, count)
    qkv_sum = fsdp_sum(qkv_parts)
    near_mine, near_other, far_mine, far_other, gain_part, grad_values = rows_call(
        after(place, qkv_parts[0]), near_normed, far_normed, far_kv_got, last_got, qkv_weight
    )
    far_rows_got = over_x((far_mine + over_core(far_other).astype(f32)).astype(bf16))
    near_rows_got = over_core(near_other)
    gain_sum = jnp.concatenate([gain_part / attention_gain, ffn_gain_part[None]], axis=0)

    def light(*pairs):
        return [join(pair) if isinstance(pair, tuple) else pair for pair in pairs]

    qkv_low, out_low = light(hold(qkv_sum, near_mine), hold(out_in, near_mine))
    qkv_in, out_across = inward(qkv_low), across(out_low)
    if two:
        gain_sum = after(gain_sum, qkv_low)
        gain_sum = gain_sum + over_core(gain_sum)
        gain_sum = gain_sum + over_x(gain_sum)
        gain_sum = gain_sum[:, :weight_rows] + over_fsdp(gain_sum[:, weight_rows:])
    qkv_low, out_low = light(hold(qkv_in, gain_sum, far_rows_got), hold(out_across, gain_sum))
    lows = [qkv_low]
    qkv_across, out_done = across(qkv_low), outward(out_low)
    if two:
        gain_sum = after(gain_sum, qkv_low)
        gain_sum = gain_sum + over_ctx(gain_sum, 1)
    (qkv_low,) = light(hold(qkv_across, gain_sum, out_done[1]))
    if two:
        gain_sum = gain_sum + over_ctx(after(gain_sum, qkv_low), 2)
    else:
        gain_sum = lax.psum(gain_sum, ("fsdp", "ctx", "tp"))
        gain_sum = lax.dynamic_slice_in_dim(gain_sum, fsdp_at * weight_rows, weight_rows, 1)
    grad_query, grad_key, grad_value = jnp.split(finish(hold(outward(qkv_low), gain_sum)), 3)
    grad_out = finish(out_done)
    grad_gate, grad_up, grad_down = first_all[:hidden].T, first_all[hidden:].T, second_all.T

    normed_grad = after(near_mine, lows[0]) + near_rows_got.astype(f32) + far_rows_got.astype(f32)
    scale = normalize(own_single)
    weighted = normed_grad * attention_gain
    grad_tokens = (
        middle_grad + scale * weighted - own_single * (scale**3 * jnp.mean(weighted * own_single, axis=-1, keepdims=True))
    )
    return (
        layer_out[:, None, :],
        relative(grad_tokens)[:, None, :],
        grad_values.reshape(4 * own_rows, 1, head_width),
        grad_query,
        grad_key,
        grad_value,
        grad_out,
        grad_gate,
        grad_up,
        grad_down,
        gain_sum[0],
        gain_sum[1],
    )

def solution(mesh):
    rows, columns = P(("ctx", "tp"), "fsdp", None), P("ctx", "fsdp", "tp")
    weight, gain = P("fsdp", "tp"), P("fsdp")
    return jax.shard_map(
        on_device,
        mesh=mesh,
        in_specs=(rows, columns, rows, P("fsdp", None), P("fsdp", None)) + (weight,) * 7 + (gain,) * 2,
        out_specs=(rows, rows, columns) + (weight,) * 7 + (gain,) * 2,
        check_vma=False,
    )
```

profile of v0, /device:TPU:0, one launch (start us, length us, event | category | flops | bytes accessed | tf_op | source)
XLA Modules:
  0.0 494.3 jit_solution(13254120289824180806)
XLA Ops:
  11.2 9.4 %collective-permute-done.1.refs_3_ = bf16[320,1024]{1,0:T(8,128)(2,1)S(1)} collective-permute-done((bf16[320,1024]{1,0:T(8,128)(2,1)S(1)}, bf16[320,1024]{1,0:T(8,128)(2,1)S(1)}, u32[]{:S(2)}, u32[]{:S(2)}) %collective-permute-start.1) | collective-permute-done | bytes 655392 | tf_op jit(solution)/shard_map/ppermute | solution.py:694
  28.0 9.9 %project.1 = (bf16[4,192,1280]{2,1,0:T(8,128)(2,1)}, bf16[640,1024]{1,0:T(8,128)(2,1)}, bf16[640,1024]{1,0:T(8,128)(2,1)}) custom-call(s32[4]{0:T(128)} %pad_add_fusion.refs_0_.refs_1_, bf16[320,1024]{1,0:T(8,128)(2,1)} %bitcast.49, bf16[320,1024]{1,0:T(8,128)(2,1)} %copy-done.22, bf16[320,1024]{1,0:T(8,128)(2,1)} %copy-done.21, ...), custom_call_target="tpu_custom_call" | custom-call | bytes 65536 | tf_op jit(solution)/shard_map/project/pallas_call | solution.py:156
  48.9 39.4 %all-to-all-done.refs_4_ = bf16[4,192,1280]{2,1,0:T(8,128)(2,1)} async-done(((bf16[4,192,1280]{2,1,0:T(8,128)(2,1)}), bf16[4,192,1280]{2,1,0:T(8,128)(2,1)}, u32[]{:S(2)}, u32[]{:S(2)}) %all-to-all-start) | async-done | bytes 1966112 | tf_op jit(solution)/shard_map/all_to_all | solution.py:703
  89.9 16.2 %attend.2 = (bf16[4,64,640]{2,1,0:T(8,128)(2,1)}, f32[4,64,640]{2,1,0:T(8,128)}, bf16[4,16,640]{2,1,0:T(8,128)(2,1)}, bf16[8,640,128]{2,1,0:T(8,128)(2,1)}, bf16...) custom-call(s32[4]{0:T(128)} %fusion.10.refs_0_, ...), custom_call_target="tpu_custom_call" | custom-call | bytes 65536 | tf_op jit(solution)/shard_map/attend/pallas_call | solution.py:156
  113.7 12.5 %attend.3 = (bf16[4,64,640]{2,1,0:T(8,128)(2,1)}, f32[4,64,640]{2,1,0:T(8,128)}, bf16[4,16,640]{2,1,0:T(8,128)(2,1)}) custom-call(s32[4]{0:T(128)} %fusion.11.refs_0_, s32[4]{0:T(128)} %pad_add_fusion.refs_0_.refs_1_, s32[8]{0:T(128)} %get-tuple-element.132.refs_2_, s32[8]{0:T(128)} %get-tuple-element.133.refs_3_, ...), custom_call_target="tpu_custom_call" | custom-call | bytes 65536 | tf_op jit(solution)/shard_map/attend/pallas_call | solution.py:156
  135.0 6.0 %collective-permute-done.7.refs_2_ = bf16[256,640]{1,0:T(8,128)(2,1)} collective-permute-done((bf16[256,640]{1,0:T(8,128)(2,1)S(1)}, bf16[256,640]{1,0:T(8,128)(2,1)}, u32[]{:S(2)}, u32[]{:S(2)}) %collective-permute-start.7) | collective-permute-done | bytes 327712 | tf_op jit(solution)/shard_map/ppermute | solution.py:694
  153.9 10.4 %feed.2 = (bf16[2,320,704]{2,1,0:T(8,128)(2,1)}, bf16[2,320,704]{2,1,0:T(8,128)(2,1)}, bf16[2,320,704]{2,1,0:T(8,128)(2,1)}, f32[320,1024]{1,0:T(8,128)}, bf16[320,1024]{1,0:T(8,128)(2,1)}) custom-call(bf16[320,1024]{1,0:T(8,128)(2,1)} %copy-done.3, bf16[320,1024]{1,0:T(8,128)(2,1)} %collective-permute-done.10.refs_1_.refs_7_, bf16[320,1024]{1,0:T(8,128)(2,1)} %copy-done, ...), custom_call_target="tpu_custom_call" | custom-call | bytes 65536 | tf_op jit(solution)/shard_map/feed/pallas_call | solution.py:156
  171.5 10.8 %feed.3 = (bf16[2,320,704]{2,1,0:T(8,128)(2,1)}, bf16[2,320,704]{2,1,0:T(8,128)(2,1)}, bf16[2,320,704]{2,1,0:T(8,128)(2,1)}, f32[320,1024]{1,0:T(8,128)}, bf16[320,1024]{1,0:T(8,128)(2,1)}) custom-call(bf16[320,1024]{1,0:T(8,128)(2,1)} %collective-permute-done.12.refs_0_.refs_8_, bf16[320,1024]{1,0:T(8,128)(2,1)} %copy-done.12, ...), custom_call_target="tpu_custom_call" | custom-call | bytes 65536 | tf_op jit(solution)/shard_map/feed/pallas_call | solution.py:156
  188.0 12.1 %feed_grads.1 = (bf16[1408,512]{1,0:T(8,128)(2,1)}, bf16[1408,512]{1,0:T(8,128)(2,1)}, bf16[704,512]{1,0:T(8,128)(2,1)}, bf16[704,512]{1,0:T(8,128)(2,1)}) custom-call(bf16[2,320,704]{2,1,0:T(8,128)(2,1)} %get-tuple-element.153.refs_0_, bf16[2,320,704]{2,1,0:T(8,128)(2,1)} %get-tuple-element.156.refs_1_, bf16[2,320,704]{2,1,0:T(8,128)(2,1)} %get-tuple-element.157.refs_2_, ...), custom_call_target="tpu_custom_call" | custom-call | bytes 65536 | tf_op jit(solution)/shard_map/feed_grads/pallas_call | solution.py:156
  220.3 8.3 %collective-permute-done.20 = bf16[256,640]{1,0:T(8,128)(2,1)} collective-permute-done((bf16[256,640]{1,0:T(8,128)(2,1)}, bf16[256,640]{1,0:T(8,128)(2,1)}, u32[]{:S(2)}, u32[]{:S(2)}) %collective-permute-start.20) | collective-permute-done | bytes 327712 | tf_op jit(solution)/shard_map/ppermute | solution.py:694
  233.5 6.5 %result.1 = (f32[320,1024]{1,0:T(8,128)}, f32[320,1024]{1,0:T(8,128)}, bf16[2,320,1024]{2,1,0:T(8,128)(2,1)}) custom-call(bf16[2,320,704]{2,1,0:T(8,128)(2,1)} %get-tuple-element.172.refs_4_.refs_0_, bf16[2,320,704]{2,1,0:T(8,128)(2,1)} %get-tuple-element.160.refs_5_.refs_1_, bf16[2368,512]{1,0:T(8,128)(2,1)} %stack.76.refs_0_.refs_4_.refs_2_, ...), custom_call_target="tpu_custom_call" | custom-call | bytes 65536 | tf_op jit(solution)/shard_map/result/pallas_call | solution.py:156
  250.3 20.4 %attend_back.3 = (bf16[2,128,640]{2,1,0:T(8,128)(2,1)}, bf16[8,128,640]{2,1,0:T(8,128)(2,1)}, bf16[8,128,640]{2,1,0:T(8,128)(2,1)}, f32[8,64,640]{2,1,0:T(8,128)}) custom-call(s32[2]{0:T(128)} %pad_add_fusion.1.refs_0_, s32[4]{0:T(128)} %pad_add_fusion.refs_0_.refs_1_, s32[8]{0:T(128)} %get-tuple-element.132.refs_2_, s32[8]{0:T(128)} %get-tuple-element.133.refs_3_, ...), custom_call_target="tpu_custom_call" | custom-call | bytes 65536 | tf_op jit(solution)/shard_map/attend_back/pallas_call | solution.py:156
  270.7 7.9 %collective-permute-done.21.refs_1_ = bf16[1408,512]{1,0:T(8,128)(2,1)} collective-permute-done((bf16[1408,512]{1,0:T(8,128)(2,1)}, bf16[1408,512]{1,0:T(8,128)(2,1)}, u32[]{:S(2)}, u32[]{:S(2)}) %collective-permute-start.21) | collective-permute-done | bytes 1441824 | tf_op jit(solution)/shard_map/ppermute | solution.py:720
  284.3 6.9 %collective-permute-start.24 = (bf16[704,512]{1,0:T(8,128)(2,1)}, bf16[704,512]{1,0:T(8,128)(2,1)}, u32[]{:S(2)}, u32[]{:S(2)}) collective-permute-start(bf16[704,512]{1,0:T(8,128)(2,1)} %get-tuple-element.194.refs_2_), channel_id=1, source_target_pairs={{0,4},{12,8},{1,5},{13,9},{2,6},{14,10},{3,7},{15,11},{16,20},{28,... | collective-permute-start | bytes 2162696 | tf_op jit(solution)/shard_map/ppermute | solution.py:720
  293.5 17.9 %attend_back.4 = (bf16[4,128,640]{2,1,0:T(8,128)(2,1)}, bf16[2,128,640]{2,1,0:T(8,128)(2,1)}, f32[8,64,640]{2,1,0:T(8,128)}) custom-call(s32[4]{0:T(128)} %pad_add_fusion.2.refs_0_, s32[4]{0:T(128)} %pad_add_fusion.refs_0_.refs_1_, s32[8]{0:T(128)} %get-tuple-element.132.refs_2_, s32[8]{0:T(128)} %get-tuple-element.133.refs_3_, ...), custom_call_target="tpu_custom_call" | custom-call | bytes 65536 | tf_op jit(solution)/shard_map/attend_back/pallas_call | solution.py:156
  318.8 12.1 %all-to-all-start.5 = ((bf16[4,128,640]{2,1,0:T(8,128)(2,1)}), bf16[4,128,640]{2,1,0:T(8,128)(2,1)}, u32[]{:S(2)}, u32[]{:S(2)}) async-start(bf16[4,128,640]{2,1,0:T(8,128)(2,1)} %get-tuple-element.213), calls=%async_computation.5 | async-start | bytes 1310720 | tf_op jit(solution)/shard_map/all_to_all | solution.py:703
  331.5 21.3 %attend_back.5 = bf16[4,256,640]{2,1,0:T(8,128)(2,1)} custom-call(s32[2]{0:T(128)} %pad_add_fusion.3.refs_0_, s32[4]{0:T(128)} %pad_add_fusion.refs_0_.refs_1_, s32[8]{0:T(128)} %get-tuple-element.132.refs_2_, s32[8]{0:T(128)} %get-tuple-element.133.refs_3_, f32[8,32,640]{2,1,0:T(8,128)} %get-tuple-element.273.refs_6_.refs_4_, ...), custom_call_target="tpu_custom_call" | custom-call | bytes 65536 | tf_op jit(solution)/shard_map/attend_back/pallas_call | solution.py:156
  372.9 17.4 %collective-permute-done.26 = bf16[704,512]{1,0:T(8,128)(2,1)} collective-permute-done((bf16[704,512]{1,0:T(8,128)(2,1)}, bf16[704,512]{1,0:T(8,128)(2,1)}, u32[]{:S(2)}, u32[]{:S(2)}) %collective-permute-start.26) | collective-permute-done | bytes 720928 | tf_op jit(solution)/shard_map/ppermute | solution.py:726
  402.7 6.1 %weight_grads.1 = (bf16[1536,256]{1,0:T(8,128)(2,1)}, bf16[1536,256]{1,0:T(8,128)(2,1)}) custom-call(bf16[640,1024]{1,0:T(8,128)(2,1)} %get-tuple-element.211.refs_0_.refs_1_, bf16[640,1024]{1,0:T(8,128)(2,1)} %get-tuple-element.212.refs_1_.refs_2_, bf16[4,128,640]{2,1,0:T(8,128)(2,1)} %all-to-all-done.5.refs_2_.refs_3_, ...), custom_call_target="tpu_custom_call" | custom-call | bytes 65536 | tf_op jit(solution)/shard_map/weight_grads/pallas_call | solution.py:156
  411.3 8.4 %rows_back.1 = (f32[320,1024]{1,0:T(8,128)}, bf16[320,1024]{1,0:T(8,128)(2,1)}, f32[320,1024]{1,0:T(8,128)}, bf16[320,1024]{1,0:T(8,128)(2,1)}, f32[1,1024]{1,0:T(1,128)}, /*index=5*/f32[2560,128]{1,0:T(8,128)}) custom-call(s32[4]{0:T(128)} %pad_add_fusion.refs_0_.refs_1_, bf16[640,1024]{1,0:T(8,128)(2,1)} %get-tuple-element.211.refs_0_.refs_1_, ...), custom_call_target="tpu_custom_call" | custom-call | bytes 65536 | tf_op jit(solution)/shard_map/rows_back/pallas_call | solution.py:156
  420.5 7.8 %collective-permute-done.33 = bf16[1536,256]{1,0:T(8,128)(2,1)} collective-permute-done((bf16[1536,256]{1,0:T(8,128)(2,1)}, bf16[1536,256]{1,0:T(8,128)(2,1)}, u32[]{:S(2)}, u32[]{:S(2)}) %collective-permute-start.33) | collective-permute-done | bytes 786464 | tf_op jit(solution)/shard_map/ppermute | solution.py:697
  442.4 6.2 %collective-permute-done.45 = bf16[512,256]{1,0:T(8,128)(2,1)S(1)} collective-permute-done((bf16[512,256]{1,0:T(8,128)(2,1)S(1)}, bf16[512,256]{1,0:T(8,128)(2,1)S(1)}, u32[]{:S(2)}, u32[]{:S(2)}) %collective-permute-start.45) | collective-permute-done | bytes 262176 | tf_op jit(solution)/shard_map/ppermute | solution.py:726
  463.0 15.0 %collective-permute-start.47 = (f32[2,512]{1,0:T(2,128)S(1)}, f32[2,512]{1,0:T(2,128)S(1)}, u32[]{:S(2)}, u32[]{:S(2)}) collective-permute-start(f32[2,512]{1,0:T(2,128)S(1)} %add.141), channel_id=1, source_target_pairs={{0,8},{4,12},{8,0},{12,4},{1,9},{5,13},{9,1},{13,5},{2,10},{6,14},... | collective-permute-start | bytes 12296 | tf_op jit(solution)/shard_map/ppermute | solution.py:700
  481.2 11.4 %collective-permute-done.46 = bf16[1536,256]{1,0:T(8,128)(2,1)S(1)} collective-permute-done((bf16[1536,256]{1,0:T(8,128)(2,1)S(1)}, bf16[1536,256]{1,0:T(8,128)(2,1)S(1)}, u32[]{:S(2)}, u32[]{:S(2)}) %collective-permute-start.46) | collective-permute-done | bytes 786464 | tf_op jit(solution)/shard_map/ppermute | solution.py:726
  (234 shorter events, 192.1 us)
Async XLA Ops:
  5.8 20.8 %collective-permute-start = (bf16[320,1024]{1,0:T(8,128)(2,1)S(1)}, bf16[320,1024]{1,0:T(8,128)(2,1)S(1)}, u32[]{:S(2)}, u32[]{:S(2)}) collective-permute-start(bf16[320,1024]{1,0:T(8,128)(2,1)S(1)} %bitcast.51), channel_id=1, source_target_pairs={{0,1},{1,0},{2,3},{3,2},{4,5},{5,4},{6,7},{7,6},{8,9},{9,8},{10,11... | collective-permute-start | bytes 1966088 | tf_op jit(solution)/shard_map/ppermute | solution.py:691
  5.9 20.8 %collective-permute-start.4 = (bf16[1536,256]{1,0:T(8,128)(2,1)}, bf16[1536,256]{1,0:T(8,128)(2,1)S(1)}, u32[]{:S(2)}, u32[]{:S(2)}) collective-permute-start(bf16[1536,256]{1,0:T(8,128)(2,1)} %stack.75.refs_9_.refs_5_), channel_id=1, source_target_pairs={{0,16},{16,0},{1,17},{17,1},{2,18},{18,2},{3,19},{19,3},{4,20},{20... | collective-permute-start | bytes 2359304 | tf_op jit(solution)/shard_map/ppermute | solution.py:697
  37.9 50.4 %all-to-all-start = ((bf16[4,192,1280]{2,1,0:T(8,128)(2,1)}), bf16[4,192,1280]{2,1,0:T(8,128)(2,1)}, u32[]{:S(2)}, u32[]{:S(2)}) async-start(bf16[4,192,1280]{2,1,0:T(8,128)(2,1)} %get-tuple-element.129), calls=%async_computation | async-start | bytes 3932160 | tf_op jit(solution)/shard_map/all_to_all | solution.py:703
  47.0 62.8 %collective-permute-start.5 = (bf16[2368,512]{1,0:T(8,128)(2,1)}, bf16[2368,512]{1,0:T(8,128)(2,1)}, u32[]{:S(2)}, u32[]{:S(2)}) collective-permute-start(bf16[2368,512]{1,0:T(8,128)(2,1)} %stack.76.refs_0_.refs_4_.refs_2_), channel_id=1, source_target_pairs={{0,16},{16,0},{1,17},{17,1},{2,18},{18,2},{3,19},{19,3},{4,20},{20... | collective-permute-start | bytes 7274504 | tf_op jit(solution)/shard_map/ppermute | solution.py:697
  88.3 25.5 %collective-permute-start.6 = (bf16[320,1024]{1,0:T(8,128)(2,1)S(1)}, bf16[320,1024]{1,0:T(8,128)(2,1)S(1)}, u32[]{:S(2)}, u32[]{:S(2)}) collective-permute-start(bf16[320,1024]{1,0:T(8,128)(2,1)S(1)} %maximum_select_fusion.2.refs_2_.refs_10_), channel_id=1, source_target_pairs={{0,2},{1,3},{2,0},{3,1},{4,6},{5,7},{6,4},{7,5},{8,10},{9,11},{10,... | collective-permute-start | bytes 1966088 | tf_op jit(solution)/shard_map/ppermute | solution.py:694
  106.1 20.1 %all-to-all-start.1 = ((bf16[4,64,640]{2,1,0:T(8,128)(2,1)}), bf16[4,64,640]{2,1,0:T(8,128)(2,1)S(1)}, u32[]{:S(2)}, u32[]{:S(2)}) async-start(bf16[4,64,640]{2,1,0:T(8,128)(2,1)} %get-tuple-element.136), calls=%async_computation.1 | async-start | bytes 655360 | tf_op jit(solution)/shard_map/all_to_all | solution.py:703
  113.1 21.9 %collective-permute-start.8 = (bf16[256,1024]{1,0:T(8,128)(2,1)}, bf16[256,1024]{1,0:T(8,128)(2,1)S(1)}, u32[]{:S(2)}, u32[]{:S(2)}) collective-permute-start(bf16[256,1024]{1,0:T(8,128)(2,1)} %pick.1.refs_3_), channel_id=1, source_target_pairs={{0,2},{1,3},{2,0},{3,1},{4,6},{5,7},{6,4},{7,5},{8,10},{9,11},{10,... | collective-permute-start | bytes 1572872 | tf_op jit(solution)/shard_map/ppermute | solution.py:694
  207.4 34.3 %collective-permute-start.16 = (bf16[1408,512]{1,0:T(8,128)(2,1)}, bf16[1408,512]{1,0:T(8,128)(2,1)}, u32[]{:S(2)}, u32[]{:S(2)}) collective-permute-start(bf16[1408,512]{1,0:T(8,128)(2,1)} %get-tuple-element.166), channel_id=1, source_target_pairs={{0,16},{16,0},{1,17},{17,1},{2,18},{18,2},{3,19},{19,3},{4,20},{20... | collective-permute-start | bytes 4325384 | tf_op jit(solution)/shard_map/ppermute | solution.py:697
  246.9 31.7 %collective-permute-start.21 = (bf16[1408,512]{1,0:T(8,128)(2,1)}, bf16[1408,512]{1,0:T(8,128)(2,1)}, u32[]{:S(2)}, u32[]{:S(2)}) collective-permute-start(bf16[1408,512]{1,0:T(8,128)(2,1)} %join.5.refs_0_), channel_id=1, source_target_pairs={{0,4},{12,8},{1,5},{13,9},{2,6},{14,10},{3,7},{15,11},{16,20},{28,... | collective-permute-start | bytes 4325384 | tf_op jit(solution)/shard_map/ppermute | solution.py:720
  249.7 21.0 %collective-permute-start.22 = (bf16[704,512]{1,0:T(8,128)(2,1)}, bf16[704,512]{1,0:T(8,128)(2,1)}, u32[]{:S(2)}, u32[]{:S(2)}) collective-permute-start(bf16[704,512]{1,0:T(8,128)(2,1)} %get-tuple-element.185), channel_id=1, source_target_pairs={{0,16},{16,0},{1,17},{17,1},{2,18},{18,2},{3,19},{19,3},{4,20},{20... | collective-permute-start | bytes 2162696 | tf_op jit(solution)/shard_map/ppermute | solution.py:697
  282.5 29.0 %collective-permute-start.23 = (bf16[1408,512]{1,0:T(8,128)(2,1)}, bf16[1408,512]{1,0:T(8,128)(2,1)}, u32[]{:S(2)}, u32[]{:S(2)}) collective-permute-start(bf16[1408,512]{1,0:T(8,128)(2,1)} %get-tuple-element.187.refs_0_), channel_id=1, source_target_pairs={{4,8},{8,4},{5,9},{9,5},{6,10},{10,6},{7,11},{11,7},{20,24},{24,20... | collective-permute-start | bytes 4325384 | tf_op jit(solution)/shard_map/ppermute | solution.py:723
  284.3 27.2 %collective-permute-start.24 = (bf16[704,512]{1,0:T(8,128)(2,1)}, bf16[704,512]{1,0:T(8,128)(2,1)}, u32[]{:S(2)}, u32[]{:S(2)}) collective-permute-start(bf16[704,512]{1,0:T(8,128)(2,1)} %get-tuple-element.194.refs_2_), channel_id=1, source_target_pairs={{0,4},{12,8},{1,5},{13,9},{2,6},{14,10},{3,7},{15,11},{16,20},{28,... | collective-permute-start | bytes 2162696 | tf_op jit(solution)/shard_map/ppermute | solution.py:720
  291.2 27.0 %collective-permute-start.27 = (bf16[320,1024]{1,0:T(8,128)(2,1)}, bf16[320,1024]{1,0:T(8,128)(2,1)}, u32[]{:S(2)}, u32[]{:S(2)}) collective-permute-start(bf16[320,1024]{1,0:T(8,128)(2,1)} %copy-done.14), channel_id=1, source_target_pairs={{0,2},{1,3},{2,0},{3,1},{4,6},{5,7},{6,4},{7,5},{8,10},{9,11},{10,... | collective-permute-start | bytes 1966088 | tf_op jit(solution)/shard_map/ppermute | solution.py:694
  292.9 67.9 %collective-permute-start.29 = (bf16[2,320,1024]{2,1,0:T(8,128)(2,1)}, bf16[2,320,1024]{2,1,0:T(8,128)(2,1)}, u32[]{:S(2)}, u32[]{:S(2)}) collective-permute-start(bf16[2,320,1024]{2,1,0:T(8,128)(2,1)} %get-tuple-element.173), channel_id=1, source_target_pairs={{0,1},{1,0},{2,3},{3,2},{4,5},{5,4},{6,7},{7,6},{8,9},{9,8},{10,11... | collective-permute-start | bytes 3932168 | tf_op jit(solution)/shard_map/ppermute | solution.py:691
  315.4 48.9 %collective-permute-start.31 = (bf16[1408,512]{1,0:T(8,128)(2,1)}, bf16[1408,512]{1,0:T(8,128)(2,1)}, u32[]{:S(2)}, u32[]{:S(2)}) collective-permute-start(bf16[1408,512]{1,0:T(8,128)(2,1)} %get-tuple-element.197), channel_id=1, source_target_pairs={{4,0},{8,12},{5,1},{9,13},{6,2},{10,14},{7,3},{11,15},{20,16},{24,... | collective-permute-start | bytes 4325384 | tf_op jit(solution)/shard_map/ppermute | solution.py:726
  316.7 36.0 %collective-permute-start.25 = (bf16[704,512]{1,0:T(8,128)(2,1)}, bf16[704,512]{1,0:T(8,128)(2,1)}, u32[]{:S(2)}, u32[]{:S(2)}) collective-permute-start(bf16[704,512]{1,0:T(8,128)(2,1)} %get-tuple-element.196.refs_0_), channel_id=1, source_target_pairs={{4,8},{8,4},{5,9},{9,5},{6,10},{10,6},{7,11},{11,7},{20,24},{24,20... | collective-permute-start | bytes 2162696 | tf_op jit(solution)/shard_map/ppermute | solution.py:723
  318.2 38.2 %collective-permute-start.28 = (bf16[320,1024]{1,0:T(8,128)(2,1)}, bf16[320,1024]{1,0:T(8,128)(2,1)}, u32[]{:S(2)}, u32[]{:S(2)}) collective-permute-start(bf16[320,1024]{1,0:T(8,128)(2,1)} %collective-permute-done.27.refs_2_), channel_id=1, source_target_pairs={{0,1},{1,0},{2,3},{3,2},{4,5},{5,4},{6,7},{7,6},{8,9},{9,8},{10,11... | collective-permute-start | bytes 1966088 | tf_op jit(solution)/shard_map/ppermute | solution.py:691
  318.8 49.1 %all-to-all-start.5 = ((bf16[4,128,640]{2,1,0:T(8,128)(2,1)}), bf16[4,128,640]{2,1,0:T(8,128)(2,1)}, u32[]{:S(2)}, u32[]{:S(2)}) async-start(bf16[4,128,640]{2,1,0:T(8,128)(2,1)} %get-tuple-element.213), calls=%async_computation.5 | async-start | bytes 1310720 | tf_op jit(solution)/shard_map/all_to_all | solution.py:703
  355.1 35.2 %collective-permute-start.26 = (bf16[704,512]{1,0:T(8,128)(2,1)}, bf16[704,512]{1,0:T(8,128)(2,1)}, u32[]{:S(2)}, u32[]{:S(2)}) collective-permute-start(bf16[704,512]{1,0:T(8,128)(2,1)} %join.8), channel_id=1, source_target_pairs={{4,0},{8,12},{5,1},{9,13},{6,2},{10,14},{7,3},{11,15},{20,16},{24,... | collective-permute-start | bytes 2162696 | tf_op jit(solution)/shard_map/ppermute | solution.py:726
  363.4 29.2 %collective-permute-start.30 = (bf16[320,1024]{1,0:T(8,128)(2,1)}, bf16[320,1024]{1,0:T(8,128)(2,1)}, u32[]{:S(2)}, u32[]{:S(2)}) collective-permute-start(bf16[320,1024]{1,0:T(8,128)(2,1)} %fusion.5), channel_id=1, source_target_pairs={{0,2},{1,3},{2,0},{3,1},{4,6},{5,7},{6,4},{7,5},{8,10},{9,11},{10,... | collective-permute-start | bytes 1966088 | tf_op jit(solution)/shard_map/ppermute | solution.py:694
  367.8 34.8 %all-to-all-start.6 = ((bf16[4,256,640]{2,1,0:T(8,128)(2,1)}), bf16[4,256,640]{2,1,0:T(8,128)(2,1)}, u32[]{:S(2)}, u32[]{:S(2)}) async-start(bf16[4,256,640]{2,1,0:T(8,128)(2,1)} %attend_back.5), calls=%async_computation.6 | async-start | bytes 2621440 | tf_op jit(solution)/shard_map/all_to_all | solution.py:703
  372.1 23.3 %collective-permute-start.32 = (bf16[512,256]{1,0:T(8,128)(2,1)S(1)}, bf16[512,256]{1,0:T(8,128)(2,1)S(1)}, u32[]{:S(2)}, u32[]{:S(2)}) collective-permute-start(bf16[512,256]{1,0:T(8,128)(2,1)S(1)} %copy-done.32), channel_id=1, source_target_pairs={{0,16},{16,0},{1,17},{17,1},{2,18},{18,2},{3,19},{19,3},{4,20},{20... | collective-permute-start | bytes 786440 | tf_op jit(solution)/shard_map/ppermute | solution.py:697
  409.8 20.3 %collective-permute-start.43 = (bf16[512,256]{1,0:T(8,128)(2,1)S(1)}, bf16[512,256]{1,0:T(8,128)(2,1)S(1)}, u32[]{:S(2)}, u32[]{:S(2)}) collective-permute-start(bf16[512,256]{1,0:T(8,128)(2,1)S(1)} %copy-done.20), channel_id=1, source_target_pairs={{0,4},{12,8},{1,5},{13,9},{2,6},{14,10},{3,7},{15,11},{16,20},{28,... | collective-permute-start | bytes 786440 | tf_op jit(solution)/shard_map/ppermute | solution.py:720
  461.6 30.9 %collective-permute-start.46 = (bf16[1536,256]{1,0:T(8,128)(2,1)S(1)}, bf16[1536,256]{1,0:T(8,128)(2,1)S(1)}, u32[]{:S(2)}, u32[]{:S(2)}) collective-permute-start(bf16[1536,256]{1,0:T(8,128)(2,1)S(1)} %add_convert_fusion), channel_id=1, source_target_pairs={{4,0},{8,12},{5,1},{9,13},{6,2},{10,14},{7,3},{11,15},{20,16},{24,... | collective-permute-start | bytes 2359304 | tf_op jit(solution)/shard_map/ppermute | solution.py:726
  (64 other events, 643.9 us)
where the time goes:
time: 504 us; the launch traced here: 494 us
  Pallas kernels  192 us (38%)
  waiting for transfers between devices  149 us (30%)
  starting transfers between devices  107 us (21%)
  other arithmetic  29.7 us (6%)
  local copies, waits for them, and re-layouts  14.2 us (3%)
    pallas_call x23, Pallas kernels, call(): pl.pallas_call(body, out_shape=outs, in_specs=[SMEM] * scalars + [pl.Bloc...  190 us
    all_to_all x7, waiting for transfers between devices, exchange(): return lax.all_to_all(by_place, 'ctx', 0, 0, tiled=True)  47.2 us
    all_to_all x7, starting transfers between devices, exchange(): return lax.all_to_all(by_place, 'ctx', 0, 0, tiled=True)  38.5 us
    ppermute x4, waiting for transfers between devices, outward(): return (low, lax.ppermute(low, 'ctx', [(1, 0), (2, 3)]))  35.9 us
    ppermute x11, waiting for transfers between devices, over_x(): return lax.ppermute(value, 'tp', [(i, i ^ 2) for i in range(tp_count)])  33.9 us
    ppermute x2, starting transfers between devices, over_ctx(): return lax.ppermute(value, 'ctx', [(i, i ^ flip) for i in range(ctx_count)])  19.3 us
    ppermute x11, starting transfers between devices, over_x(): return lax.ppermute(value, 'tp', [(i, i ^ 2) for i in range(tp_count)])  19.1 us
    ppermute x4, starting transfers between devices, inward(): return (low, lax.ppermute(low, 'ctx', [(0, 1), (3, 2)]))  12.6 us
  transfers between devices with their start and end apart: 55, of which 27 were waited for; matrix products, arithmetic and copies ran while one was open for 6% of the time, Pallas kernels for 31%

commit v1 on v0

--- a/solution.py
+++ b/solution.py
@@ -341,15 +341,19 @@
             grads_out[at] = jnp.concatenate([grad[p], three_parts(delta), pad], axis=0)
 
 
-def by_projection(kv, last):
-    columns = kv.shape[0] * HEAD
-    flat = lambda ref, at: ref[:, at * HEAD : (at + 1) * HEAD, :].reshape(columns, ref.shape[2])
-    return (flat(last, 2), flat(last, 0), flat(last, 1)), (flat(last, 3), flat(kv, 0), flat(kv, 1))
-
-
-def weights_kernel(near_rows, far_rows, kv, last, *parts):
-    size = near_rows.shape[1] // len(parts)
-    near, far = by_projection(kv, last)
+def by_projection(got):
+    columns = got.shape[0] * HEAD
+    flat = lambda at: got[:, at * HEAD : (at + 1) * HEAD, :].reshape(columns, got.shape[2])
+    return (flat(2), flat(0), flat(1)), (flat(3), flat(4), flat(5))
+
+
+def weights_kernel(near_rows, far_rows, last, *rest):
+    count = len(rest) // 2
+    out_parts, parts = rest[:count], rest[count:]
+    size = near_rows.shape[1] // count
+    for part, out_part in zip(parts, out_parts):
+        part[3 * size :, :] = out_part[...]
+    near, far = by_projection(last)
     for i in range(3):
         for b, part in enumerate(parts):
             lanes = slice(b * size, (b + 1) * size)
@@ -357,18 +361,18 @@
             part[i * size : (i + 1) * size, :] = sums.T.astype(bf16)
 
 
-def weights_call(near_rows, far_rows, kv, last, count):
-    width, columns = near_rows.shape[1], kv.shape[0] * HEAD
+def weights_call(near_rows, far_rows, last, out_parts):
+    width, columns, count = near_rows.shape[1], last.shape[0] * HEAD, len(out_parts)
     return call(
-        weights_kernel, "weight_grads", tuple(shape_of(3 * width // count, columns) for _ in range(count)),
-        (near_rows, far_rows, kv, last), scalars=0,
-    )
-
-
-def rows_kernel(place_ref, near_rows, far_rows, kv, last, *rest, count):
+        weights_kernel, "weight_grads", tuple(shape_of(4 * width // count, columns) for _ in range(count)),
+        (near_rows, far_rows, last, *out_parts), scalars=0,
+    )
+
+
+def rows_kernel(place_ref, near_rows, far_rows, last, *rest, count):
     weights, (near_mine, near_other, far_mine, far_other, gain_ref, value_ref, total) = rest[:count], rest[count:]
     size = near_rows.shape[1] // count
-    near, far = by_projection(kv, last)
+    near, far = by_projection(last)
     for half, grads in enumerate((near, far)):
         value = grads[2].T.astype(f32)
         tokens, columns = value.shape
@@ -387,14 +391,14 @@
         split_core(place_ref, total, mine, other)
 
 
-def rows_call(place, near_rows, far_rows, kv, last, weights):
+def rows_call(place, near_rows, far_rows, last, weights):
     size, width = near_rows.shape
     rows = (shape_of(size // 2, width, dtype=f32), shape_of(size // 2, width))
-    values = shape_of(2 * size * kv.shape[0] * HEAD // 128, 128, dtype=f32)
+    values = shape_of(2 * size * last.shape[0] * HEAD // 128, 128, dtype=f32)
     return call(
         functools.partial(rows_kernel, count=len(weights)), "rows_back",
         rows + rows + (shape_of(1, width, dtype=f32), values),
-        (place, near_rows, far_rows, kv, last, *weights),
+        (place, near_rows, far_rows, last, *weights),
         scratch=[pltpu.VMEM((size, width), f32)],
     )
 
@@ -404,24 +408,28 @@
     count = len(outs) // 2
     size = rows[0].shape[1] // count
     hidden = near_gate.shape[2]
+    half = hidden // 2
     pairs = ((near_gate, far_gate, rows), (near_up, far_up, rows), (near_hidden, far_hidden, cots))
     for b in range(count):
         lanes = slice(b * size, (b + 1) * size)
+        first, second = outs[b], outs[count + b]
         for i, (near, far, right) in enumerate(pairs):
             near, far = (ref[...].reshape(2 * ref.shape[1], hidden) for ref in (near, far))
             near_right, far_right = (jnp.concatenate([right[j][:, lanes], right[j + 1][:, lanes]], axis=0) for j in (0, 2))
             total = (dot(near, near_right, 0, 0) + dot(far, far_right, 0, 0)).astype(bf16)
-            if i < 2:
-                outs[b][i * hidden : (i + 1) * hidden, :] = total
+            if i == 0:
+                first[:hidden, :] = total
+            elif i == 1:
+                first[hidden:, :] = total[:half]
+                second[:half, :] = total[half:]
             else:
-                outs[count + b][...] = total
+                second[half:, :] = total
 
 
 def feed_grads_call(lefts, hiddens, rows, cots, count):
     hidden, size = lefts[0].shape[2], rows[0].shape[1] // count
     outs = call(
-        feed_grads_kernel, "feed_grads",
-        (shape_of(2 * hidden, size),) * count + (shape_of(hidden, size),) * count,
+        feed_grads_kernel, "feed_grads", tuple(shape_of(3 * hidden // 2, size) for _ in range(2 * count)),
         (*lefts, *hiddens, *rows, *cots), scalars=0, mib=40,
     )
     return outs[:count], outs[count:]
@@ -584,19 +592,17 @@
         grads, kept, sum_in, rest = rest[0], rest[1], rest[2], rest[3:]
     else:
         before, rest = rest[:6], rest[6:]
-    outs, rest = rest[: (4, 3, 1)[stage]], rest[(4, 3, 1)[stage] :]
+    outs, rest = rest[: (4, 1)[stage]], rest[(4, 1)[stage] :]
     if not stage:
         prep_back(place_ref, queries, *before, outs[1], outs[2], extra)
         queries, grads = outs[1], outs[2]
     score_a, grad_a, score_b, grad_b, key_sum, value_sum, todo = rest[:7]
-    sums = rest[7] if stage == 2 else outs[-1]
+    sums = rest[7] if stage else outs[-1]
     pieces = queries.shape[0]
     scores, prob_grads = (score_a, score_b), (grad_a, grad_b)
     sums[...] = sum_in[...] if stage else jnp.zeros(sums.shape, f32)
-    if stage == 1:
-        outs[0][:2] = kept[...]
-    if stage == 2:
-        outs[0][2:, : 2 * HEAD, :] = kept[...]
+    if stage:
+        outs[0][:, 4 * HEAD :, :] = kept[...]
     ready()
 
     def attend(i, carry):
@@ -624,19 +630,12 @@
         key_grad = unrotate(key_sum[...] * (1.0 / LOG2E), cos_ref[at], sin_ref[at]).astype(bf16)
         value_grad = (0.5 * value_sum[...]).astype(bf16)
 
-        def write(ref, place):
-            ref[place, :HEAD, :] = key_grad
-            ref[place, HEAD : 2 * HEAD, :] = value_grad
-
-        if stage == 1:
-            pl.when(i < 2)(lambda: write(outs[0], 2 + i))
-            pl.when(i >= 2)(lambda: write(outs[1], i - 2))
-        else:
-            write(outs[0], i)
+        outs[0][i, :HEAD, :] = key_grad
+        outs[0][i, HEAD : 2 * HEAD, :] = value_grad
         return carry
 
     lax.fori_loop(0, todo_count, attend, 0)
-    if stage == 2:
+    if stage:
         for p in range(pieces):
             grad = unrotate(sums[p] * SCORE_SCALE, cos_ref[p], sin_ref[p]).astype(bf16)
             start = pl.multiple_of((2 + ((p % 2) ^ place_ref[0])) * HEAD, HEAD)
@@ -648,9 +647,8 @@
     places = pieces // 2
     sums = shape_of(pieces, HEAD, piece, dtype=f32)
     outs = (
-        (shape_of(2, 2 * HEAD, piece), shape_of(*queries.shape), shape_of(*queries.shape), sums),
-        (shape_of(places, 2 * HEAD, piece), shape_of(2, 2 * HEAD, piece), sums),
-        (shape_of(places, 4 * HEAD, piece),),
+        (shape_of(places, 2 * HEAD, piece), shape_of(*queries.shape), shape_of(*queries.shape), sums),
+        (shape_of(places, 6 * HEAD, piece),),
     )[stage]
     operands = (cosine, sine, keys, key_lanes, values, queries, *more)
     got = call(
@@ -659,10 +657,10 @@
         scratch=[pltpu.VMEM((piece, piece), f32)] * 4
         + [pltpu.VMEM((HEAD, piece), f32)] * 2
         + [pltpu.SMEM((pieces,), jnp.int32)]
-        + ([pltpu.VMEM(sums.shape, f32)] if stage == 2 else []),
+        + ([pltpu.VMEM(sums.shape, f32)] if stage else []),
         scalars=4, mib=36, late=(0, 1),
     )
-    return got[0] if stage == 2 else got
+    return got[0] if stage else got
 
 
 def after(value, *earlier):
@@ -852,39 +850,27 @@
         )
 
     far_at, near_at = [2 * i + 1 - x_at for i in range(4)], [2 * i + x_at for i in range(4)]
-    first_kv, back_queries, grads, query_sum = back(
-        0, far_at[:2], (queries, near_grads, far_grads, near_full, far_full, near_lse, far_lse), first_low
-    )
-
-    first_low, second_low = step(hold(first_in, first_kv), hold(second_sum, first_kv))
+    far_kv, back_queries, grads, query_sum = back(
+        0, far_at, (queries, near_grads, far_grads, near_full, far_full, near_lse, far_lse), first_low
+    )
+
+    first_low, second_low = step(hold(first_in, far_kv), hold(second_sum, far_kv))
     first_across, second_in = across(first_low), inward(second_low)
-    far_kv, near_kv, query_sum = back(
-        1, far_at[2:] + near_at[2:], (back_queries, grads, first_kv, query_sum), first_low
-    )
-
-    first_low, second_low = step(hold(first_across, far_kv), hold(second_in, far_kv))
+    last = back(1, near_at, (back_queries, grads, far_kv, query_sum), first_low)
+    first_got, second_got = hold(first_across, last), hold(second_in, last)
+
+    last_got = exchange(last)
+    out_parts = out_grads_call(after(place, last), chip_low, low_x, low_x_core, near_mixed, far_mixed, count)
+    far_result_got = over_x((after(far_result, out_parts[0]) + sent_got[1].astype(f32)).astype(bf16))
+    layer_out = relative((middle + near_result + sent_got[0].astype(f32) + far_result_got.astype(f32)).astype(bf16))
+    last_got = after(last_got, layer_out)
+
+    qkv_parts = weights_call(near_normed, far_normed, last_got, out_parts)
+    qkv_sum = fsdp_sum(qkv_parts)
+    first_low, second_low = step(hold(first_got, qkv_parts[0]), hold(second_got, qkv_parts[0]))
     first_done, second_across = outward(first_low), across(second_low)
-    far_kv_got = exchange(after(far_kv, first_low))
-    last = back(2, near_at[:2], (back_queries, grads, near_kv, query_sum), first_low)
-
-    (second_low,) = step(hold(second_across, last))
-    second_done = outward(second_low)
-    last_got = exchange(after(last, second_low, first_done[1]))
-    far_kv_got = after(far_kv_got, last)
-    out_parts = out_grads_call(after(place, last), chip_low, low_x, low_x_core, near_mixed, far_mixed, count)
-    out_sum = fsdp_sum(out_parts)
-    far_result_got = over_x((after(far_result, out_parts[0]) + sent_got[1].astype(f32)).astype(bf16))
-    second_all = finish(hold(second_done, out_parts[0]))
-    layer_out = relative((after(middle, second_all) + near_result + sent_got[0].astype(f32) + far_result_got.astype(f32)).astype(bf16))
-    first_all = finish(hold(first_done, second_low))
-    (out_low,) = step(hold(out_sum, layer_out))
-    last_got = after(last_got, first_all, out_low)
-    out_in = inward(out_low)
-
-    qkv_parts = weights_call(near_normed, far_normed, far_kv_got, last_got, count)
-    qkv_sum = fsdp_sum(qkv_parts)
     near_mine, near_other, far_mine, far_other, gain_part, grad_values = rows_call(
-        after(place, qkv_parts[0]), near_normed, far_normed, far_kv_got, last_got, qkv_weight
+        after(place, first_low), near_normed, far_normed, last_got, qkv_weight
     )
     far_rows_got = over_x((far_mine + over_core(far_other).astype(f32)).astype(bf16))
     near_rows_got = over_core(near_other)
@@ -893,28 +879,30 @@
     def light(*pairs):
         return [join(pair) if isinstance(pair, tuple) else pair for pair in pairs]
 
-    qkv_low, out_low = light(hold(qkv_sum, near_mine), hold(out_in, near_mine))
-    qkv_in, out_across = inward(qkv_low), across(out_low)
+    qkv_low, second_low = light(hold(qkv_sum, near_mine), hold(second_across, near_mine))
+    qkv_in, second_done = inward(qkv_low), outward(second_low)
+    first_all = finish(hold(first_done, qkv_in[1] if isinstance(qkv_in, tuple) else qkv_in))
     if two:
         gain_sum = after(gain_sum, qkv_low)
         gain_sum = gain_sum + over_core(gain_sum)
         gain_sum = gain_sum + over_x(gain_sum)
         gain_sum = gain_sum[:, :weight_rows] + over_fsdp(gain_sum[:, weight_rows:])
-    qkv_low, out_low = light(hold(qkv_in, gain_sum, far_rows_got), hold(out_across, gain_sum))
+    (qkv_low,) = light(hold(qkv_in, gain_sum, far_rows_got, first_all))
     lows = [qkv_low]
-    qkv_across, out_done = across(qkv_low), outward(out_low)
+    qkv_across = across(qkv_low)
     if two:
         gain_sum = after(gain_sum, qkv_low)
         gain_sum = gain_sum + over_ctx(gain_sum, 1)
-    (qkv_low,) = light(hold(qkv_across, gain_sum, out_done[1]))
+    second_all = finish(hold(second_done, qkv_across[1]))
+    (qkv_low,) = light(hold(qkv_across, gain_sum, second_all))
     if two:
         gain_sum = gain_sum + over_ctx(after(gain_sum, qkv_low), 2)
     else:
         gain_sum = lax.psum(gain_sum, ("fsdp", "ctx", "tp"))
         gain_sum = lax.dynamic_slice_in_dim(gain_sum, fsdp_at * weight_rows, weight_rows, 1)
-    grad_query, grad_key, grad_value = jnp.split(finish(hold(outward(qkv_low), gain_sum)), 3)
-    grad_out = finish(out_done)
-    grad_gate, grad_up, grad_down = first_all[:hidden].T, first_all[hidden:].T, second_all.T
+    grad_query, grad_key, grad_value, grad_out = jnp.split(finish(hold(outward(qkv_low), gain_sum)), 4)
+    grad_gate, grad_down = first_all[:hidden].T, second_all[hidden // 2 :].T
+    grad_up = jnp.concatenate([first_all[hidden:], second_all[: hidden // 2]], axis=0).T
 
     normed_grad = after(near_mine, lows[0]) + near_rows_got.astype(f32) + far_rows_got.astype(f32)
     scale = normalize(own_single)

time: 504 us -> 496 us (0.984)
  waiting for transfers between devices: 149 us -> 168 us
  starting transfers between devices: 107 us -> 91.2 us
  Pallas kernels: 192 us -> 183 us
    all_to_all x7 -> x6, waiting for transfers between devices: 47.2 us -> 61.1 us  [exchange(): return lax.all_to_all(by_place, 'ctx', 0, 0, tiled=True)]
    ppermute x2, waiting for transfers between devices: 0.3 us -> 13.1 us  [over_ctx(): return lax.ppermute(value, 'ctx', [(i, i ^ flip) for i in range(ctx_count)])]
    all_to_all x7 -> x6, starting transfers between devices: 38.5 us -> 27.5 us  [exchange(): return lax.all_to_all(by_place, 'ctx', 0, 0, tiled=True)]
    pallas_call x23 -> x20, Pallas kernels: 190 us -> 180 us  [call(): pl.pallas_call(body, out_shape=outs, in_specs=[SMEM] * scalars + [pl.Bloc...]
    ppermute x4 -> x3, waiting for transfers between devices: 35.9 us -> 27 us  [outward(): return (low, lax.ppermute(low, 'ctx', [(1, 0), (2, 3)]))]
    ppermute x4 -> x3, waiting for transfers between devices: 11.1 us -> 3.82 us  [inward(): return (low, lax.ppermute(low, 'ctx', [(0, 1), (3, 2)]))]
    ppermute x11, waiting for transfers between devices: 33.9 us -> 40.9 us  [over_x(): return lax.ppermute(value, 'tp', [(i, i ^ 2) for i in range(tp_count)])]
    ppermute x4 -> x3, starting transfers between devices: 12.6 us -> 19.4 us  [inward(): return (low, lax.ppermute(low, 'ctx', [(0, 1), (3, 2)]))]
  transfers between devices with their start and end apart: 55 -> 50, of which waited for: 27 -> 25; matrix products, arithmetic and copies ran while one was open for 6% -> 6% of each run, Pallas kernels for 31% -> 32%
where the time goes in v1:
time: 496 us; the launch traced here: 488 us
  Pallas kernels  183 us (37%)
  waiting for transfers between devices  168 us (34%)
  starting transfers between devices  91.2 us (18%)
  other arithmetic  28.2 us (6%)
  local copies, waits for them, and re-layouts  15.4 us (3%)
    pallas_call x20, Pallas kernels, call(): pl.pallas_call(body, out_shape=outs, in_specs=[SMEM] * scalars + [pl.Bloc...  180 us
    all_to_all x6, waiting for transfers between devices, exchange(): return lax.all_to_all(by_place, 'ctx', 0, 0, tiled=True)  61.1 us
    ppermute x11, waiting for transfers between devices, over_x(): return lax.ppermute(value, 'tp', [(i, i ^ 2) for i in range(tp_count)])  40.9 us
    all_to_all x6, starting transfers between devices, exchange(): return lax.all_to_all(by_place, 'ctx', 0, 0, tiled=True)  27.5 us
    ppermute x3, waiting for transfers between devices, outward(): return (low, lax.ppermute(low, 'ctx', [(1, 0), (2, 3)]))  27 us
    ppermute x3, starting transfers between devices, inward(): return (low, lax.ppermute(low, 'ctx', [(0, 1), (3, 2)]))  19.4 us
    ppermute x11, starting transfers between devices, over_x(): return lax.ppermute(value, 'tp', [(i, i ^ 2) for i in range(tp_count)])  16.7 us
    ppermute x2, starting transfers between devices, over_ctx(): return lax.ppermute(value, 'ctx', [(i, i ^ flip) for i in range(ctx_count)])  13.7 us
  transfers between devices with their start and end apart: 50, of which 25 were waited for; matrix products, arithmetic and copies ran while one was open for 6% of the time, Pallas kernels for 32%

profile of v1, /device:TPU:0, one launch (start us, length us, event | category | flops | bytes accessed | tf_op | source)
XLA Modules:
  0.0 487.6 jit_solution(797794610660462564)
XLA Ops:
  11.2 9.4 %collective-permute-done.1.refs_3_ = bf16[320,1024]{1,0:T(8,128)(2,1)S(1)} collective-permute-done((bf16[320,1024]{1,0:T(8,128)(2,1)S(1)}, bf16[320,1024]{1,0:T(8,128)(2,1)S(1)}, u32[]{:S(2)}, u32[]{:S(2)}) %collective-permute-start.1) | collective-permute-done | bytes 655392 | tf_op jit(solution)/shard_map/ppermute | solution.py:692
  28.0 9.9 %project.1 = (bf16[4,192,1280]{2,1,0:T(8,128)(2,1)}, bf16[640,1024]{1,0:T(8,128)(2,1)}, bf16[640,1024]{1,0:T(8,128)(2,1)}) custom-call(s32[4]{0:T(128)} %pad_add_fusion.refs_0_.refs_1_, bf16[320,1024]{1,0:T(8,128)(2,1)} %bitcast.50, bf16[320,1024]{1,0:T(8,128)(2,1)} %copy-done.23, bf16[320,1024]{1,0:T(8,128)(2,1)} %copy-done.22, ...), custom_call_target="tpu_custom_call" | custom-call | bytes 65536 | tf_op jit(solution)/shard_map/project/pallas_call | solution.py:156
  50.0 38.3 %all-to-all-done.refs_4_ = bf16[4,192,1280]{2,1,0:T(8,128)(2,1)} async-done(((bf16[4,192,1280]{2,1,0:T(8,128)(2,1)}), bf16[4,192,1280]{2,1,0:T(8,128)(2,1)}, u32[]{:S(2)}, u32[]{:S(2)}) %all-to-all-start) | async-done | bytes 1966112 | tf_op jit(solution)/shard_map/all_to_all | solution.py:701
  89.9 16.3 %attend.2 = (bf16[4,64,640]{2,1,0:T(8,128)(2,1)}, f32[4,64,640]{2,1,0:T(8,128)}, bf16[4,16,640]{2,1,0:T(8,128)(2,1)}, bf16[8,640,128]{2,1,0:T(8,128)(2,1)}, bf16...) custom-call(s32[4]{0:T(128)} %fusion.10.refs_0_, ...), custom_call_target="tpu_custom_call" | custom-call | bytes 65536 | tf_op jit(solution)/shard_map/attend/pallas_call | solution.py:156
  116.1 12.5 %attend.3 = (bf16[4,64,640]{2,1,0:T(8,128)(2,1)}, f32[4,64,640]{2,1,0:T(8,128)}, bf16[4,16,640]{2,1,0:T(8,128)(2,1)}) custom-call(s32[4]{0:T(128)} %fusion.11.refs_0_, s32[4]{0:T(128)} %pad_add_fusion.refs_0_.refs_1_, s32[8]{0:T(128)} %get-tuple-element.123.refs_2_, s32[8]{0:T(128)} %get-tuple-element.124.refs_3_, ...), custom_call_target="tpu_custom_call" | custom-call | bytes 65536 | tf_op jit(solution)/shard_map/attend/pallas_call | solution.py:156
  137.4 6.2 %collective-permute-done.7.refs_2_ = bf16[256,640]{1,0:T(8,128)(2,1)S(1)} collective-permute-done((bf16[256,640]{1,0:T(8,128)(2,1)}, bf16[256,640]{1,0:T(8,128)(2,1)S(1)}, u32[]{:S(2)}, u32[]{:S(2)}) %collective-permute-start.7) | collective-permute-done | bytes 327712 | tf_op jit(solution)/shard_map/ppermute | solution.py:692
  156.3 10.4 %feed.2 = (bf16[2,320,704]{2,1,0:T(8,128)(2,1)}, bf16[2,320,704]{2,1,0:T(8,128)(2,1)}, bf16[2,320,704]{2,1,0:T(8,128)(2,1)}, f32[320,1024]{1,0:T(8,128)}, bf16[320,1024]{1,0:T(8,128)(2,1)}) custom-call(bf16[320,1024]{1,0:T(8,128)(2,1)} %copy-done.4, bf16[320,1024]{1,0:T(8,128)(2,1)} %collective-permute-done.10.refs_1_.refs_7_, bf16[320,1024]{1,0:T(8,128)(2,1)} %copy-done.1, ...), custom_call_target="tpu_custom_call" | custom-call | bytes 65536 | tf_op jit(solution)/shard_map/feed/pallas_call | solution.py:156
  173.9 10.7 %feed.3 = (bf16[2,320,704]{2,1,0:T(8,128)(2,1)}, bf16[2,320,704]{2,1,0:T(8,128)(2,1)}, bf16[2,320,704]{2,1,0:T(8,128)(2,1)}, f32[320,1024]{1,0:T(8,128)}, bf16[320,1024]{1,0:T(8,128)(2,1)}) custom-call(bf16[320,1024]{1,0:T(8,128)(2,1)} %collective-permute-done.13.refs_0_.refs_8_, bf16[320,1024]{1,0:T(8,128)(2,1)} %copy-done.13, ...), custom_call_target="tpu_custom_call" | custom-call | bytes 65536 | tf_op jit(solution)/shard_map/feed/pallas_call | solution.py:156
  190.3 12.2 %feed_grads.1 = (bf16[1056,512]{1,0:T(8,128)(2,1)}, bf16[1056,512]{1,0:T(8,128)(2,1)}, bf16[1056,512]{1,0:T(8,128)(2,1)}, bf16[1056,512]{1,0:T(8,128)(2,1)}) custom-call(bf16[2,320,704]{2,1,0:T(8,128)(2,1)} %get-tuple-element.150.refs_0_, bf16[2,320,704]{2,1,0:T(8,128)(2,1)} %get-tuple-element.151.refs_1_, bf16[2,320,704]{2,1,0:T(8,128)(2,1)} %get-tuple-element.152.refs_2_, ...), custom_call_target="tpu_custom_call" | custom-call | bytes 65536 | tf_op jit(solution)/shard_map/feed_grads/pallas_call | solution.py:156
  222.4 8.3 %collective-permute-done.21 = bf16[256,640]{1,0:T(8,128)(2,1)} collective-permute-done((bf16[256,640]{1,0:T(8,128)(2,1)}, bf16[256,640]{1,0:T(8,128)(2,1)}, u32[]{:S(2)}, u32[]{:S(2)}) %collective-permute-start.21) | collective-permute-done | bytes 327712 | tf_op jit(solution)/shard_map/ppermute | solution.py:692
  235.7 6.5 %result.1 = (f32[320,1024]{1,0:T(8,128)}, f32[320,1024]{1,0:T(8,128)}, bf16[2,320,1024]{2,1,0:T(8,128)(2,1)}) custom-call(bf16[2,320,704]{2,1,0:T(8,128)(2,1)} %get-tuple-element.160.refs_4_.refs_0_, bf16[2,320,704]{2,1,0:T(8,128)(2,1)} %get-tuple-element.154.refs_5_.refs_1_, bf16[2368,512]{1,0:T(8,128)(2,1)} %stack.72.refs_0_.refs_4_.refs_2_, ...), custom_call_target="tpu_custom_call" | custom-call | bytes 65536 | tf_op jit(solution)/shard_map/result/pallas_call | solution.py:156
  254.2 25.7 %attend_back.2 = (bf16[4,128,640]{2,1,0:T(8,128)(2,1)}, bf16[8,128,640]{2,1,0:T(8,128)(2,1)}, bf16[8,128,640]{2,1,0:T(8,128)(2,1)}, f32[8,64,640]{2,1,0:T(8,128)}) custom-call(s32[4]{0:T(128)} %pad_add_fusion.2.refs_0_, s32[4]{0:T(128)} %pad_add_fusion.refs_0_.refs_1_, s32[8]{0:T(128)} %get-tuple-element.123.refs_2_, s32[8]{0:T(128)} %get-tuple-element.124.refs_3_, ...), custom_call_target="tpu_custom_call" | custom-call | bytes 65536 | tf_op jit(solution)/shard_map/attend_back/pallas_call | solution.py:156
  283.8 28.7 %attend_back.3 = bf16[4,384,640]{2,1,0:T(8,128)(2,1)} custom-call(s32[4]{0:T(128)} %pad_add_fusion.1.refs_0_, s32[4]{0:T(128)} %pad_add_fusion.refs_0_.refs_1_, s32[8]{0:T(128)} %get-tuple-element.123.refs_2_, s32[8]{0:T(128)} %get-tuple-element.124.refs_3_, f32[8,32,640]{2,1,0:T(8,128)} %get-tuple-element.256.refs_6_.refs_4_, ...), custom_call_target="tpu_custom_call" | custom-call | bytes 65536 | tf_op jit(solution)/shard_map/attend_back/pallas_call | solution.py:156
  327.8 6.8 %collective-permute-start.28 = (bf16[1056,512]{1,0:T(8,128)(2,1)}, bf16[1056,512]{1,0:T(8,128)(2,1)}, u32[]{:S(2)}, u32[]{:S(2)}) collective-permute-start(bf16[1056,512]{1,0:T(8,128)(2,1)} %get-tuple-element.197.refs_2_), channel_id=1, source_target_pairs={{0,4},{12,8},{1,5},{13,9},{2,6},{14,10},{3,7},{15,11},{16,20},{28,... | collective-permute-start | bytes 3244040 | tf_op jit(solution)/shard_map/ppermute | solution.py:718
  334.5 8.1 %collective-permute-done.26 = bf16[320,1024]{1,0:T(8,128)(2,1)S(1)} collective-permute-done((bf16[320,1024]{1,0:T(8,128)(2,1)S(1)}, bf16[320,1024]{1,0:T(8,128)(2,1)S(1)}, u32[]{:S(2)}, u32[]{:S(2)}) %collective-permute-start.26) | collective-permute-done | bytes 655392 | tf_op jit(solution)/shard_map/ppermute | solution.py:692
  345.3 18.5 %all-to-all-done.5.refs_2_.refs_3_ = bf16[4,384,640]{2,1,0:T(8,128)(2,1)} async-done(((bf16[4,384,640]{2,1,0:T(8,128)(2,1)}), bf16[4,384,640]{2,1,0:T(8,128)(2,1)}, u32[]{:S(2)}, u32[]{:S(2)}) %all-to-all-start.5) | async-done | bytes 1966112 | tf_op jit(solution)/shard_map/all_to_all | solution.py:701
  363.8 6.4 %weight_grads.1 = (bf16[2048,256]{1,0:T(8,128)(2,1)}, bf16[2048,256]{1,0:T(8,128)(2,1)}) custom-call(bf16[640,1024]{1,0:T(8,128)(2,1)} %get-tuple-element.191.refs_0_.refs_1_, bf16[640,1024]{1,0:T(8,128)(2,1)} %get-tuple-element.192.refs_1_.refs_2_, bf16[4,384,640]{2,1,0:T(8,128)(2,1)} %all-to-all-done.5.refs_2_.refs_3_, ...), custom_call_target="tpu_custom_call" | custom-call | bytes 65536 | tf_op jit(solution)/shard_map/weight_grads/pallas_call | solution.py:156
  376.6 8.4 %rows_back.1 = (f32[320,1024]{1,0:T(8,128)}, bf16[320,1024]{1,0:T(8,128)(2,1)}, f32[320,1024]{1,0:T(8,128)}, bf16[320,1024]{1,0:T(8,128)(2,1)}, f32[1,1024]{1,0:T(1,128)}, /*index=5*/f32[2560,128]{1,0:T(8,128)}) custom-call(s32[4]{0:T(128)} %pad_add_fusion.refs_0_.refs_1_, bf16[640,1024]{1,0:T(8,128)(2,1)} %get-tuple-element.191.refs_0_.refs_1_, ...), custom_call_target="tpu_custom_call" | custom-call | bytes 65536 | tf_op jit(solution)/shard_map/rows_back/pallas_call | solution.py:156
  387.4 7.0 %collective-permute-done.29 = bf16[2048,256]{1,0:T(8,128)(2,1)} collective-permute-done((bf16[2048,256]{1,0:T(8,128)(2,1)}, bf16[2048,256]{1,0:T(8,128)(2,1)}, u32[]{:S(2)}, u32[]{:S(2)}) %collective-permute-start.29) | collective-permute-done | bytes 1048608 | tf_op jit(solution)/shard_map/ppermute | solution.py:695
  402.0 10.0 %collective-permute-start.30 = (bf16[2048,256]{1,0:T(8,128)(2,1)}, bf16[2048,256]{1,0:T(8,128)(2,1)S(1)}, u32[]{:S(2)}, u32[]{:S(2)}) collective-permute-start(bf16[2048,256]{1,0:T(8,128)(2,1)} %add_convert_fusion.3), channel_id=1, source_target_pairs={{0,4},{12,8},{1,5},{13,9},{2,6},{14,10},{3,7},{15,11},{16,20},{28,... | collective-permute-start | bytes 3145736 | tf_op jit(solution)/shard_map/ppermute | solution.py:718
  419.1 13.7 %collective-permute-done.36 = bf16[1056,512]{1,0:T(8,128)(2,1)S(1)} collective-permute-done((bf16[1056,512]{1,0:T(8,128)(2,1)}, bf16[1056,512]{1,0:T(8,128)(2,1)S(1)}, u32[]{:S(2)}, u32[]{:S(2)}) %collective-permute-start.36) | collective-permute-done | bytes 1081376 | tf_op jit(solution)/shard_map/ppermute | solution.py:724
  442.2 13.1 %collective-permute-done.39 = f32[2,512]{1,0:T(2,128)S(1)} collective-permute-done((f32[2,512]{1,0:T(2,128)S(1)}, f32[2,512]{1,0:T(2,128)S(1)}, u32[]{:S(2)}, u32[]{:S(2)}) %collective-permute-start.39) | collective-permute-done | bytes 4128 | tf_op jit(solution)/shard_map/ppermute | solution.py:698
  461.3 8.5 %collective-permute-start.43 = (f32[2,512]{1,0:T(2,128)S(1)}, f32[2,512]{1,0:T(2,128)S(1)}, u32[]{:S(2)}, u32[]{:S(2)}) collective-permute-start(f32[2,512]{1,0:T(2,128)S(1)} %add.138), channel_id=1, source_target_pairs={{0,8},{4,12},{8,0},{12,4},{1,9},{5,13},{9,1},{13,5},{2,10},{6,14},... | collective-permute-start | bytes 12296 | tf_op jit(solution)/shard_map/ppermute | solution.py:698
  472.3 13.3 %collective-permute-done.42 = bf16[2048,256]{1,0:T(8,128)(2,1)S(1)} collective-permute-done((bf16[2048,256]{1,0:T(8,128)(2,1)S(1)}, bf16[2048,256]{1,0:T(8,128)(2,1)S(1)}, u32[]{:S(2)}, u32[]{:S(2)}) %collective-permute-start.42) | collective-permute-done | bytes 1048608 | tf_op jit(solution)/shard_map/ppermute | solution.py:724
  (217 shorter events, 176.8 us)
Async XLA Ops:
  5.8 20.8 %collective-permute-start = (bf16[320,1024]{1,0:T(8,128)(2,1)S(1)}, bf16[320,1024]{1,0:T(8,128)(2,1)S(1)}, u32[]{:S(2)}, u32[]{:S(2)}) collective-permute-start(bf16[320,1024]{1,0:T(8,128)(2,1)S(1)} %bitcast.52), channel_id=1, source_target_pairs={{0,1},{1,0},{2,3},{3,2},{4,5},{5,4},{6,7},{7,6},{8,9},{9,8},{10,11... | collective-permute-start | bytes 1966088 | tf_op jit(solution)/shard_map/ppermute | solution.py:689
  5.8 20.8 %collective-permute-start.4 = (bf16[1536,256]{1,0:T(8,128)(2,1)}, bf16[1536,256]{1,0:T(8,128)(2,1)S(1)}, u32[]{:S(2)}, u32[]{:S(2)}) collective-permute-start(bf16[1536,256]{1,0:T(8,128)(2,1)} %stack.71.refs_9_.refs_4_), channel_id=1, source_target_pairs={{0,16},{16,0},{1,17},{17,1},{2,18},{18,2},{3,19},{19,3},{4,20},{20... | collective-permute-start | bytes 2359304 | tf_op jit(solution)/shard_map/ppermute | solution.py:695
  37.8 50.4 %all-to-all-start = ((bf16[4,192,1280]{2,1,0:T(8,128)(2,1)}), bf16[4,192,1280]{2,1,0:T(8,128)(2,1)}, u32[]{:S(2)}, u32[]{:S(2)}) async-start(bf16[4,192,1280]{2,1,0:T(8,128)(2,1)} %get-tuple-element.120), calls=%async_computation | async-start | bytes 3932160 | tf_op jit(solution)/shard_map/all_to_all | solution.py:701
  47.1 63.8 %collective-permute-start.5 = (bf16[2368,512]{1,0:T(8,128)(2,1)}, bf16[2368,512]{1,0:T(8,128)(2,1)S(1)}, u32[]{:S(2)}, u32[]{:S(2)}) collective-permute-start(bf16[2368,512]{1,0:T(8,128)(2,1)} %stack.72.refs_0_.refs_4_.refs_2_), channel_id=1, source_target_pairs={{0,16},{16,0},{1,17},{17,1},{2,18},{18,2},{3,19},{19,3},{4,20},{20... | collective-permute-start | bytes 7274504 | tf_op jit(solution)/shard_map/ppermute | solution.py:695
  88.2 27.9 %collective-permute-start.6 = (bf16[320,1024]{1,0:T(8,128)(2,1)S(1)}, bf16[320,1024]{1,0:T(8,128)(2,1)}, u32[]{:S(2)}, u32[]{:S(2)}) collective-permute-start(bf16[320,1024]{1,0:T(8,128)(2,1)S(1)} %maximum_select_fusion.2.refs_2_.refs_10_), channel_id=1, source_target_pairs={{0,2},{1,3},{2,0},{3,1},{4,6},{5,7},{6,4},{7,5},{8,10},{9,11},{10,... | collective-permute-start | bytes 1966088 | tf_op jit(solution)/shard_map/ppermute | solution.py:692
  106.2 22.5 %all-to-all-start.1 = ((bf16[4,64,640]{2,1,0:T(8,128)(2,1)}), bf16[4,64,640]{2,1,0:T(8,128)(2,1)}, u32[]{:S(2)}, u32[]{:S(2)}) async-start(bf16[4,64,640]{2,1,0:T(8,128)(2,1)} %get-tuple-element.127), calls=%async_computation.1 | async-start | bytes 655360 | tf_op jit(solution)/shard_map/all_to_all | solution.py:701
  115.5 21.9 %collective-permute-start.8 = (bf16[256,1024]{1,0:T(8,128)(2,1)}, bf16[256,1024]{1,0:T(8,128)(2,1)S(1)}, u32[]{:S(2)}, u32[]{:S(2)}) collective-permute-start(bf16[256,1024]{1,0:T(8,128)(2,1)} %pick.1.refs_3_), channel_id=1, source_target_pairs={{0,2},{1,3},{2,0},{3,1},{4,6},{5,7},{6,4},{7,5},{8,10},{9,11},{10,... | collective-permute-start | bytes 1572872 | tf_op jit(solution)/shard_map/ppermute | solution.py:692
  209.5 32.7 %collective-permute-start.20 = (bf16[1056,512]{1,0:T(8,128)(2,1)}, bf16[1056,512]{1,0:T(8,128)(2,1)}, u32[]{:S(2)}, u32[]{:S(2)}) collective-permute-start(bf16[1056,512]{1,0:T(8,128)(2,1)} %get-tuple-element.164), channel_id=1, source_target_pairs={{0,16},{16,0},{1,17},{17,1},{2,18},{18,2},{3,19},{19,3},{4,20},{20... | collective-permute-start | bytes 3244040 | tf_op jit(solution)/shard_map/ppermute | solution.py:695
  235.6 44.3 %collective-permute-start.23 = (bf16[1056,512]{1,0:T(8,128)(2,1)}, bf16[1056,512]{1,0:T(8,128)(2,1)}, u32[]{:S(2)}, u32[]{:S(2)}) collective-permute-start(bf16[1056,512]{1,0:T(8,128)(2,1)} %get-tuple-element.178), channel_id=1, source_target_pairs={{0,16},{16,0},{1,17},{17,1},{2,18},{18,2},{3,19},{19,3},{4,20},{20... | collective-permute-start | bytes 3244040 | tf_op jit(solution)/shard_map/ppermute | solution.py:695
  248.6 31.4 %collective-permute-start.22 = (bf16[1056,512]{1,0:T(8,128)(2,1)}, bf16[1056,512]{1,0:T(8,128)(2,1)}, u32[]{:S(2)}, u32[]{:S(2)}) collective-permute-start(bf16[1056,512]{1,0:T(8,128)(2,1)} %join.3.refs_0_), channel_id=1, source_target_pairs={{0,4},{12,8},{1,5},{13,9},{2,6},{14,10},{3,7},{15,11},{16,20},{28,... | collective-permute-start | bytes 3244040 | tf_op jit(solution)/shard_map/ppermute | solution.py:718
  251.3 72.7 %collective-permute-start.19 = (bf16[2,320,1024]{2,1,0:T(8,128)(2,1)}, bf16[2,320,1024]{2,1,0:T(8,128)(2,1)}, u32[]{:S(2)}, u32[]{:S(2)}) collective-permute-start(bf16[2,320,1024]{2,1,0:T(8,128)(2,1)} %get-tuple-element.162), channel_id=1, source_target_pairs={{0,1},{1,0},{2,3},{3,2},{4,5},{5,4},{6,7},{7,6},{8,9},{9,8},{10,11... | collective-permute-start | bytes 3932168 | tf_op jit(solution)/shard_map/ppermute | solution.py:689
  251.3 65.7 %collective-permute-start.24 = (bf16[320,1024]{1,0:T(8,128)(2,1)}, bf16[320,1024]{1,0:T(8,128)(2,1)}, u32[]{:S(2)}, u32[]{:S(2)}) collective-permute-start(bf16[320,1024]{1,0:T(8,128)(2,1)} %copy-done.16), channel_id=1, source_target_pairs={{0,2},{1,3},{2,0},{3,1},{4,6},{5,7},{6,4},{7,5},{8,10},{9,11},{10,... | collective-permute-start | bytes 1966088 | tf_op jit(solution)/shard_map/ppermute | solution.py:692
  312.5 51.3 %all-to-all-start.5 = ((bf16[4,384,640]{2,1,0:T(8,128)(2,1)}), bf16[4,384,640]{2,1,0:T(8,128)(2,1)}, u32[]{:S(2)}, u32[]{:S(2)}) async-start(bf16[4,384,640]{2,1,0:T(8,128)(2,1)} %attend_back.3), calls=%async_computation.5 | async-start | bytes 3932160 | tf_op jit(solution)/shard_map/all_to_all | solution.py:701
  326.1 46.6 %collective-permute-start.27 = (bf16[1056,512]{1,0:T(8,128)(2,1)}, bf16[1056,512]{1,0:T(8,128)(2,1)}, u32[]{:S(2)}, u32[]{:S(2)}) collective-permute-start(bf16[1056,512]{1,0:T(8,128)(2,1)} %get-tuple-element.180.refs_0_), channel_id=1, source_target_pairs={{4,8},{8,4},{5,9},{9,5},{6,10},{10,6},{7,11},{11,7},{20,24},{24,20... | collective-permute-start | bytes 3244040 | tf_op jit(solution)/shard_map/ppermute | solution.py:721
  327.8 45.0 %collective-permute-start.28 = (bf16[1056,512]{1,0:T(8,128)(2,1)}, bf16[1056,512]{1,0:T(8,128)(2,1)}, u32[]{:S(2)}, u32[]{:S(2)}) collective-permute-start(bf16[1056,512]{1,0:T(8,128)(2,1)} %get-tuple-element.197.refs_2_), channel_id=1, source_target_pairs={{0,4},{12,8},{1,5},{13,9},{2,6},{14,10},{3,7},{15,11},{16,20},{28,... | collective-permute-start | bytes 3244040 | tf_op jit(solution)/shard_map/ppermute | solution.py:718
  370.3 24.1 %collective-permute-start.29 = (bf16[2048,256]{1,0:T(8,128)(2,1)}, bf16[2048,256]{1,0:T(8,128)(2,1)}, u32[]{:S(2)}, u32[]{:S(2)}) collective-permute-start(bf16[2048,256]{1,0:T(8,128)(2,1)} %get-tuple-element.203), channel_id=1, source_target_pairs={{0,16},{16,0},{1,17},{17,1},{2,18},{18,2},{3,19},{19,3},{4,20},{20... | collective-permute-start | bytes 3145736 | tf_op jit(solution)/shard_map/ppermute | solution.py:695
  385.0 27.0 %collective-permute-start.34 = (bf16[320,1024]{1,0:T(8,128)(2,1)}, bf16[320,1024]{1,0:T(8,128)(2,1)}, u32[]{:S(2)}, u32[]{:S(2)}) collective-permute-start(bf16[320,1024]{1,0:T(8,128)(2,1)} %get-tuple-element.209), channel_id=1, source_target_pairs={{0,1},{1,0},{2,3},{3,2},{4,5},{5,4},{6,7},{7,6},{8,9},{9,8},{10,11... | collective-permute-start | bytes 1966088 | tf_op jit(solution)/shard_map/ppermute | solution.py:689
  385.1 30.9 %collective-permute-start.40 = (bf16[1056,512]{1,0:T(8,128)(2,1)}, bf16[1056,512]{1,0:T(8,128)(2,1)}, u32[]{:S(2)}, u32[]{:S(2)}) collective-permute-start(bf16[1056,512]{1,0:T(8,128)(2,1)} %get-tuple-element.216), channel_id=1, source_target_pairs={{4,8},{8,4},{5,9},{9,5},{6,10},{10,6},{7,11},{11,7},{20,24},{24,20... | collective-permute-start | bytes 3244040 | tf_op jit(solution)/shard_map/ppermute | solution.py:721
  398.7 34.1 %collective-permute-start.36 = (bf16[1056,512]{1,0:T(8,128)(2,1)}, bf16[1056,512]{1,0:T(8,128)(2,1)S(1)}, u32[]{:S(2)}, u32[]{:S(2)}) collective-permute-start(bf16[1056,512]{1,0:T(8,128)(2,1)} %get-tuple-element.200), channel_id=1, source_target_pairs={{4,0},{8,12},{5,1},{9,13},{6,2},{10,14},{7,3},{11,15},{20,16},{24,... | collective-permute-start | bytes 3244040 | tf_op jit(solution)/shard_map/ppermute | solution.py:724
  399.9 40.9 %collective-permute-start.37 = (bf16[320,1024]{1,0:T(8,128)(2,1)}, bf16[320,1024]{1,0:T(8,128)(2,1)S(1)}, u32[]{:S(2)}, u32[]{:S(2)}) collective-permute-start(bf16[320,1024]{1,0:T(8,128)(2,1)} %get-tuple-element.213), channel_id=1, source_target_pairs={{0,1},{1,0},{2,3},{3,2},{4,5},{5,4},{6,7},{7,6},{8,9},{9,8},{10,11... | collective-permute-start | bytes 1966088 | tf_op jit(solution)/shard_map/ppermute | solution.py:689
  402.0 32.2 %collective-permute-start.30 = (bf16[2048,256]{1,0:T(8,128)(2,1)}, bf16[2048,256]{1,0:T(8,128)(2,1)S(1)}, u32[]{:S(2)}, u32[]{:S(2)}) collective-permute-start(bf16[2048,256]{1,0:T(8,128)(2,1)} %add_convert_fusion.3), channel_id=1, source_target_pairs={{0,4},{12,8},{1,5},{13,9},{2,6},{14,10},{3,7},{15,11},{16,20},{28,... | collective-permute-start | bytes 3145736 | tf_op jit(solution)/shard_map/ppermute | solution.py:718
  417.7 37.7 %collective-permute-start.41 = (bf16[1056,512]{1,0:T(8,128)(2,1)S(1)}, bf16[1056,512]{1,0:T(8,128)(2,1)S(1)}, u32[]{:S(2)}, u32[]{:S(2)}) collective-permute-start(bf16[1056,512]{1,0:T(8,128)(2,1)S(1)} %add_convert_fusion), channel_id=1, source_target_pairs={{4,0},{8,12},{5,1},{9,13},{6,2},{10,14},{7,3},{11,15},{20,16},{24,... | collective-permute-start | bytes 3244040 | tf_op jit(solution)/shard_map/ppermute | solution.py:724
  434.7 20.6 %collective-permute-start.38 = (bf16[2048,256]{1,0:T(8,128)(2,1)S(1)}, bf16[2048,256]{1,0:T(8,128)(2,1)S(1)}, u32[]{:S(2)}, u32[]{:S(2)}) collective-permute-start(bf16[2048,256]{1,0:T(8,128)(2,1)S(1)} %add_convert_fusion.2), channel_id=1, source_target_pairs={{4,8},{8,4},{5,9},{9,5},{6,10},{10,6},{7,11},{11,7},{20,24},{24,20... | collective-permute-start | bytes 3145736 | tf_op jit(solution)/shard_map/ppermute | solution.py:721
  455.8 29.8 %collective-permute-start.42 = (bf16[2048,256]{1,0:T(8,128)(2,1)S(1)}, bf16[2048,256]{1,0:T(8,128)(2,1)S(1)}, u32[]{:S(2)}, u32[]{:S(2)}) collective-permute-start(bf16[2048,256]{1,0:T(8,128)(2,1)S(1)} %add_convert_fusion.1), channel_id=1, source_target_pairs={{4,0},{8,12},{5,1},{9,13},{6,2},{10,14},{7,3},{11,15},{20,16},{24,... | collective-permute-start | bytes 3145736 | tf_op jit(solution)/shard_map/ppermute | solution.py:724
  (58 other events, 554.5 us)

commit v2 on v1

--- a/solution.py
+++ b/solution.py
@@ -231,15 +231,34 @@
 
 
 def pick_kernel(*refs):
-    out = refs[-1]
-    rows = out.shape[0]
-    size = out.shape[1] // (len(refs) - 1)
-    for i, ref in enumerate(refs[:-1]):
-        out[:, i * size : (i + 1) * size] = ref[ref.shape[0] - rows :, :]
+    out, inside, sems = refs[-3:]
+    blocks, rows = refs[:-3], out.shape[0]
+    size = out.shape[1] // len(blocks)
+    copies = [
+        pltpu.make_async_copy(ref.at[pl.ds(ref.shape[0] - rows, rows), :], inside.at[:, pl.ds(i * size, size)], sems.at[i])
+        for i, ref in enumerate(blocks)
+    ]
+    for copy in copies:
+        copy.start()
+    for copy in copies:
+        copy.wait()
+    copy = pltpu.make_async_copy(inside, out, sems.at[len(blocks)])
+    copy.start()
+    copy.wait()
 
 
 def pick_call(blocks, rows):
-    return call(pick_kernel, "pick", shape_of(rows, blocks[0].shape[1] * len(blocks)), tuple(blocks), scalars=0)
+    out = shape_of(rows, blocks[0].shape[1] * len(blocks))
+    return pl.pallas_call(
+        pick_kernel,
+        out_shape=out,
+        in_specs=[pl.BlockSpec(memory_space=pltpu.HBM)] * len(blocks),
+        out_specs=pl.BlockSpec(memory_space=pltpu.HBM),
+        scratch_shapes=[pltpu.VMEM(out.shape, out.dtype), pltpu.SemaphoreType.DMA((len(blocks) + 1,))],
+        compiler_params=pltpu.CompilerParams(vmem_limit_bytes=60 << 20),
+        cost_estimate=pl.CostEstimate(flops=0, bytes_accessed=1 << 16, transcendentals=0),
+        name="pick",
+    )(*blocks)
 
 
 def stack_call(*arrays):

time: 496 us -> 490 us (0.988)
    pallas_call x20 -> x19, Pallas kernels: 180 us -> 177 us  [call(): pl.pallas_call(body, out_shape=outs, in_specs=[SMEM] * scalars + [pl.Bloc...]
where the time goes in v2:
time: 490 us; the launch traced here: 486 us
  Pallas kernels  181 us (37%)
  waiting for transfers between devices  168 us (34%)
  starting transfers between devices  91.2 us (19%)
  other arithmetic  28.2 us (6%)
  local copies, waits for them, and re-layouts  15.4 us (3%)
    pallas_call x19, Pallas kernels, call(): pl.pallas_call(body, out_shape=outs, in_specs=[SMEM] * scalars + [pl.Bloc...  177 us
    all_to_all x6, waiting for transfers between devices, exchange(): return lax.all_to_all(by_place, 'ctx', 0, 0, tiled=True)  61.1 us
    ppermute x11, waiting for transfers between devices, over_x(): return lax.ppermute(value, 'tp', [(i, i ^ 2) for i in range(tp_count)])  40.9 us
    all_to_all x6, starting transfers between devices, exchange(): return lax.all_to_all(by_place, 'ctx', 0, 0, tiled=True)  27.5 us
    ppermute x3, waiting for transfers between devices, outward(): return (low, lax.ppermute(low, 'ctx', [(1, 0), (2, 3)]))  27 us
    ppermute x3, starting transfers between devices, inward(): return (low, lax.ppermute(low, 'ctx', [(0, 1), (3, 2)]))  19.4 us
    ppermute x11, starting transfers between devices, over_x(): return lax.ppermute(value, 'tp', [(i, i ^ 2) for i in range(tp_count)])  16.7 us
    ppermute x2, starting transfers between devices, over_ctx(): return lax.ppermute(value, 'ctx', [(i, i ^ flip) for i in range(ctx_count)])  13.7 us
  transfers between devices with their start and end apart: 50, of which 25 were waited for; matrix products, arithmetic and copies ran while one was open for 6% of the time, Pallas kernels for 32%

profile of v2, /device:TPU:0, one launch (start us, length us, event | category | flops | bytes accessed | tf_op | source)
XLA Modules:
  0.0 486.1 jit_solution(10103258028750464111)
XLA Ops:
  11.2 9.4 %collective-permute-done.1.refs_3_ = bf16[320,1024]{1,0:T(8,128)(2,1)S(1)} collective-permute-done((bf16[320,1024]{1,0:T(8,128)(2,1)S(1)}, bf16[320,1024]{1,0:T(8,128)(2,1)S(1)}, u32[]{:S(2)}, u32[]{:S(2)}) %collective-permute-start.1) | collective-permute-done | bytes 655392 | tf_op jit(solution)/shard_map/ppermute | solution.py:711
  28.0 9.9 %project.1 = (bf16[4,192,1280]{2,1,0:T(8,128)(2,1)}, bf16[640,1024]{1,0:T(8,128)(2,1)}, bf16[640,1024]{1,0:T(8,128)(2,1)}) custom-call(s32[4]{0:T(128)} %pad_add_fusion.refs_0_.refs_1_, bf16[320,1024]{1,0:T(8,128)(2,1)} %bitcast.50, bf16[320,1024]{1,0:T(8,128)(2,1)} %copy-done.23, bf16[320,1024]{1,0:T(8,128)(2,1)} %copy-done.22, ...), custom_call_target="tpu_custom_call" | custom-call | bytes 65536 | tf_op jit(solution)/shard_map/project/pallas_call | solution.py:156
  50.0 38.3 %all-to-all-done.refs_4_ = bf16[4,192,1280]{2,1,0:T(8,128)(2,1)} async-done(((bf16[4,192,1280]{2,1,0:T(8,128)(2,1)}), bf16[4,192,1280]{2,1,0:T(8,128)(2,1)}, u32[]{:S(2)}, u32[]{:S(2)}) %all-to-all-start) | async-done | bytes 1966112 | tf_op jit(solution)/shard_map/all_to_all | solution.py:720
  89.9 16.3 %attend.2 = (bf16[4,64,640]{2,1,0:T(8,128)(2,1)}, f32[4,64,640]{2,1,0:T(8,128)}, bf16[4,16,640]{2,1,0:T(8,128)(2,1)}, bf16[8,640,128]{2,1,0:T(8,128)(2,1)}, bf16...) custom-call(s32[4]{0:T(128)} %fusion.10.refs_0_, ...), custom_call_target="tpu_custom_call" | custom-call | bytes 65536 | tf_op jit(solution)/shard_map/attend/pallas_call | solution.py:156
  114.7 12.5 %attend.3 = (bf16[4,64,640]{2,1,0:T(8,128)(2,1)}, f32[4,64,640]{2,1,0:T(8,128)}, bf16[4,16,640]{2,1,0:T(8,128)(2,1)}) custom-call(s32[4]{0:T(128)} %fusion.11.refs_0_, s32[4]{0:T(128)} %pad_add_fusion.refs_0_.refs_1_, s32[8]{0:T(128)} %get-tuple-element.123.refs_2_, s32[8]{0:T(128)} %get-tuple-element.124.refs_3_, ...), custom_call_target="tpu_custom_call" | custom-call | bytes 65536 | tf_op jit(solution)/shard_map/attend/pallas_call | solution.py:156
  136.0 6.2 %collective-permute-done.7.refs_2_ = bf16[256,640]{1,0:T(8,128)(2,1)S(1)} collective-permute-done((bf16[256,640]{1,0:T(8,128)(2,1)}, bf16[256,640]{1,0:T(8,128)(2,1)S(1)}, u32[]{:S(2)}, u32[]{:S(2)}) %collective-permute-start.7) | collective-permute-done | bytes 327712 | tf_op jit(solution)/shard_map/ppermute | solution.py:711
  154.9 10.4 %feed.2 = (bf16[2,320,704]{2,1,0:T(8,128)(2,1)}, bf16[2,320,704]{2,1,0:T(8,128)(2,1)}, bf16[2,320,704]{2,1,0:T(8,128)(2,1)}, f32[320,1024]{1,0:T(8,128)}, bf16[320,1024]{1,0:T(8,128)(2,1)}) custom-call(bf16[320,1024]{1,0:T(8,128)(2,1)} %copy-done.4, bf16[320,1024]{1,0:T(8,128)(2,1)} %collective-permute-done.10.refs_1_.refs_7_, bf16[320,1024]{1,0:T(8,128)(2,1)} %copy-done.1, ...), custom_call_target="tpu_custom_call" | custom-call | bytes 65536 | tf_op jit(solution)/shard_map/feed/pallas_call | solution.py:156
  172.5 10.7 %feed.3 = (bf16[2,320,704]{2,1,0:T(8,128)(2,1)}, bf16[2,320,704]{2,1,0:T(8,128)(2,1)}, bf16[2,320,704]{2,1,0:T(8,128)(2,1)}, f32[320,1024]{1,0:T(8,128)}, bf16[320,1024]{1,0:T(8,128)(2,1)}) custom-call(bf16[320,1024]{1,0:T(8,128)(2,1)} %collective-permute-done.13.refs_0_.refs_8_, bf16[320,1024]{1,0:T(8,128)(2,1)} %copy-done.13, ...), custom_call_target="tpu_custom_call" | custom-call | bytes 65536 | tf_op jit(solution)/shard_map/feed/pallas_call | solution.py:156
  188.9 12.2 %feed_grads.1 = (bf16[1056,512]{1,0:T(8,128)(2,1)}, bf16[1056,512]{1,0:T(8,128)(2,1)}, bf16[1056,512]{1,0:T(8,128)(2,1)}, bf16[1056,512]{1,0:T(8,128)(2,1)}) custom-call(bf16[2,320,704]{2,1,0:T(8,128)(2,1)} %get-tuple-element.150.refs_0_, bf16[2,320,704]{2,1,0:T(8,128)(2,1)} %get-tuple-element.151.refs_1_, bf16[2,320,704]{2,1,0:T(8,128)(2,1)} %get-tuple-element.152.refs_2_, ...), custom_call_target="tpu_custom_call" | custom-call | bytes 65536 | tf_op jit(solution)/shard_map/feed_grads/pallas_call | solution.py:156
  221.0 8.3 %collective-permute-done.21 = bf16[256,640]{1,0:T(8,128)(2,1)} collective-permute-done((bf16[256,640]{1,0:T(8,128)(2,1)}, bf16[256,640]{1,0:T(8,128)(2,1)}, u32[]{:S(2)}, u32[]{:S(2)}) %collective-permute-start.21) | collective-permute-done | bytes 327712 | tf_op jit(solution)/shard_map/ppermute | solution.py:711
  234.2 6.5 %result.1 = (f32[320,1024]{1,0:T(8,128)}, f32[320,1024]{1,0:T(8,128)}, bf16[2,320,1024]{2,1,0:T(8,128)(2,1)}) custom-call(bf16[2,320,704]{2,1,0:T(8,128)(2,1)} %get-tuple-element.160.refs_4_.refs_0_, bf16[2,320,704]{2,1,0:T(8,128)(2,1)} %get-tuple-element.154.refs_5_.refs_1_, bf16[2368,512]{1,0:T(8,128)(2,1)} %stack.72.refs_0_.refs_4_.refs_2_, ...), custom_call_target="tpu_custom_call" | custom-call | bytes 65536 | tf_op jit(solution)/shard_map/result/pallas_call | solution.py:156
  252.8 25.7 %attend_back.2 = (bf16[4,128,640]{2,1,0:T(8,128)(2,1)}, bf16[8,128,640]{2,1,0:T(8,128)(2,1)}, bf16[8,128,640]{2,1,0:T(8,128)(2,1)}, f32[8,64,640]{2,1,0:T(8,128)}) custom-call(s32[4]{0:T(128)} %pad_add_fusion.2.refs_0_, s32[4]{0:T(128)} %pad_add_fusion.refs_0_.refs_1_, s32[8]{0:T(128)} %get-tuple-element.123.refs_2_, s32[8]{0:T(128)} %get-tuple-element.124.refs_3_, ...), custom_call_target="tpu_custom_call" | custom-call | bytes 65536 | tf_op jit(solution)/shard_map/attend_back/pallas_call | solution.py:156
  282.4 28.7 %attend_back.3 = bf16[4,384,640]{2,1,0:T(8,128)(2,1)} custom-call(s32[4]{0:T(128)} %pad_add_fusion.1.refs_0_, s32[4]{0:T(128)} %pad_add_fusion.refs_0_.refs_1_, s32[8]{0:T(128)} %get-tuple-element.123.refs_2_, s32[8]{0:T(128)} %get-tuple-element.124.refs_3_, f32[8,32,640]{2,1,0:T(8,128)} %get-tuple-element.256.refs_6_.refs_4_, ...), custom_call_target="tpu_custom_call" | custom-call | bytes 65536 | tf_op jit(solution)/shard_map/attend_back/pallas_call | solution.py:156
  326.3 6.8 %collective-permute-start.28 = (bf16[1056,512]{1,0:T(8,128)(2,1)}, bf16[1056,512]{1,0:T(8,128)(2,1)}, u32[]{:S(2)}, u32[]{:S(2)}) collective-permute-start(bf16[1056,512]{1,0:T(8,128)(2,1)} %get-tuple-element.197.refs_2_), channel_id=1, source_target_pairs={{0,4},{12,8},{1,5},{13,9},{2,6},{14,10},{3,7},{15,11},{16,20},{28,... | collective-permute-start | bytes 3244040 | tf_op jit(solution)/shard_map/ppermute | solution.py:737
  333.1 8.1 %collective-permute-done.26 = bf16[320,1024]{1,0:T(8,128)(2,1)S(1)} collective-permute-done((bf16[320,1024]{1,0:T(8,128)(2,1)S(1)}, bf16[320,1024]{1,0:T(8,128)(2,1)S(1)}, u32[]{:S(2)}, u32[]{:S(2)}) %collective-permute-start.26) | collective-permute-done | bytes 655392 | tf_op jit(solution)/shard_map/ppermute | solution.py:711
  343.9 18.5 %all-to-all-done.5.refs_2_.refs_3_ = bf16[4,384,640]{2,1,0:T(8,128)(2,1)} async-done(((bf16[4,384,640]{2,1,0:T(8,128)(2,1)}), bf16[4,384,640]{2,1,0:T(8,128)(2,1)}, u32[]{:S(2)}, u32[]{:S(2)}) %all-to-all-start.5) | async-done | bytes 1966112 | tf_op jit(solution)/shard_map/all_to_all | solution.py:720
  362.4 6.4 %weight_grads.1 = (bf16[2048,256]{1,0:T(8,128)(2,1)}, bf16[2048,256]{1,0:T(8,128)(2,1)}) custom-call(bf16[640,1024]{1,0:T(8,128)(2,1)} %get-tuple-element.191.refs_0_.refs_1_, bf16[640,1024]{1,0:T(8,128)(2,1)} %get-tuple-element.192.refs_1_.refs_2_, bf16[4,384,640]{2,1,0:T(8,128)(2,1)} %all-to-all-done.5.refs_2_.refs_3_, ...), custom_call_target="tpu_custom_call" | custom-call | bytes 65536 | tf_op jit(solution)/shard_map/weight_grads/pallas_call | solution.py:156
  375.2 8.4 %rows_back.1 = (f32[320,1024]{1,0:T(8,128)}, bf16[320,1024]{1,0:T(8,128)(2,1)}, f32[320,1024]{1,0:T(8,128)}, bf16[320,1024]{1,0:T(8,128)(2,1)}, f32[1,1024]{1,0:T(1,128)}, /*index=5*/f32[2560,128]{1,0:T(8,128)}) custom-call(s32[4]{0:T(128)} %pad_add_fusion.refs_0_.refs_1_, bf16[640,1024]{1,0:T(8,128)(2,1)} %get-tuple-element.191.refs_0_.refs_1_, ...), custom_call_target="tpu_custom_call" | custom-call | bytes 65536 | tf_op jit(solution)/shard_map/rows_back/pallas_call | solution.py:156
  386.0 7.0 %collective-permute-done.29 = bf16[2048,256]{1,0:T(8,128)(2,1)} collective-permute-done((bf16[2048,256]{1,0:T(8,128)(2,1)}, bf16[2048,256]{1,0:T(8,128)(2,1)}, u32[]{:S(2)}, u32[]{:S(2)}) %collective-permute-start.29) | collective-permute-done | bytes 1048608 | tf_op jit(solution)/shard_map/ppermute | solution.py:714
  400.6 10.0 %collective-permute-start.30 = (bf16[2048,256]{1,0:T(8,128)(2,1)}, bf16[2048,256]{1,0:T(8,128)(2,1)S(1)}, u32[]{:S(2)}, u32[]{:S(2)}) collective-permute-start(bf16[2048,256]{1,0:T(8,128)(2,1)} %add_convert_fusion.3), channel_id=1, source_target_pairs={{0,4},{12,8},{1,5},{13,9},{2,6},{14,10},{3,7},{15,11},{16,20},{28,... | collective-permute-start | bytes 3145736 | tf_op jit(solution)/shard_map/ppermute | solution.py:737
  417.7 13.7 %collective-permute-done.36 = bf16[1056,512]{1,0:T(8,128)(2,1)S(1)} collective-permute-done((bf16[1056,512]{1,0:T(8,128)(2,1)}, bf16[1056,512]{1,0:T(8,128)(2,1)S(1)}, u32[]{:S(2)}, u32[]{:S(2)}) %collective-permute-start.36) | collective-permute-done | bytes 1081376 | tf_op jit(solution)/shard_map/ppermute | solution.py:743
  440.8 13.1 %collective-permute-done.39 = f32[2,512]{1,0:T(2,128)S(1)} collective-permute-done((f32[2,512]{1,0:T(2,128)S(1)}, f32[2,512]{1,0:T(2,128)S(1)}, u32[]{:S(2)}, u32[]{:S(2)}) %collective-permute-start.39) | collective-permute-done | bytes 4128 | tf_op jit(solution)/shard_map/ppermute | solution.py:717
  459.8 8.5 %collective-permute-start.43 = (f32[2,512]{1,0:T(2,128)S(1)}, f32[2,512]{1,0:T(2,128)S(1)}, u32[]{:S(2)}, u32[]{:S(2)}) collective-permute-start(f32[2,512]{1,0:T(2,128)S(1)} %add.138), channel_id=1, source_target_pairs={{0,8},{4,12},{8,0},{12,4},{1,9},{5,13},{9,1},{13,5},{2,10},{6,14},... | collective-permute-start | bytes 12296 | tf_op jit(solution)/shard_map/ppermute | solution.py:717
  470.8 13.3 %collective-permute-done.42 = bf16[2048,256]{1,0:T(8,128)(2,1)S(1)} collective-permute-done((bf16[2048,256]{1,0:T(8,128)(2,1)S(1)}, bf16[2048,256]{1,0:T(8,128)(2,1)S(1)}, u32[]{:S(2)}, u32[]{:S(2)}) %collective-permute-start.42) | collective-permute-done | bytes 1048608 | tf_op jit(solution)/shard_map/ppermute | solution.py:743
  (217 shorter events, 175.3 us)
Async XLA Ops:
  5.8 20.8 %collective-permute-start = (bf16[320,1024]{1,0:T(8,128)(2,1)S(1)}, bf16[320,1024]{1,0:T(8,128)(2,1)S(1)}, u32[]{:S(2)}, u32[]{:S(2)}) collective-permute-start(bf16[320,1024]{1,0:T(8,128)(2,1)S(1)} %bitcast.52), channel_id=1, source_target_pairs={{0,1},{1,0},{2,3},{3,2},{4,5},{5,4},{6,7},{7,6},{8,9},{9,8},{10,11... | collective-permute-start | bytes 1966088 | tf_op jit(solution)/shard_map/ppermute | solution.py:708
  5.8 20.8 %collective-permute-start.4 = (bf16[1536,256]{1,0:T(8,128)(2,1)}, bf16[1536,256]{1,0:T(8,128)(2,1)S(1)}, u32[]{:S(2)}, u32[]{:S(2)}) collective-permute-start(bf16[1536,256]{1,0:T(8,128)(2,1)} %stack.71.refs_9_.refs_4_), channel_id=1, source_target_pairs={{0,16},{16,0},{1,17},{17,1},{2,18},{18,2},{3,19},{19,3},{4,20},{20... | collective-permute-start | bytes 2359304 | tf_op jit(solution)/shard_map/ppermute | solution.py:714
  37.8 50.4 %all-to-all-start = ((bf16[4,192,1280]{2,1,0:T(8,128)(2,1)}), bf16[4,192,1280]{2,1,0:T(8,128)(2,1)}, u32[]{:S(2)}, u32[]{:S(2)}) async-start(bf16[4,192,1280]{2,1,0:T(8,128)(2,1)} %get-tuple-element.120), calls=%async_computation | async-start | bytes 3932160 | tf_op jit(solution)/shard_map/all_to_all | solution.py:720
  47.1 63.8 %collective-permute-start.5 = (bf16[2368,512]{1,0:T(8,128)(2,1)}, bf16[2368,512]{1,0:T(8,128)(2,1)S(1)}, u32[]{:S(2)}, u32[]{:S(2)}) collective-permute-start(bf16[2368,512]{1,0:T(8,128)(2,1)} %stack.72.refs_0_.refs_4_.refs_2_), channel_id=1, source_target_pairs={{0,16},{16,0},{1,17},{17,1},{2,18},{18,2},{3,19},{19,3},{4,20},{20... | collective-permute-start | bytes 7274504 | tf_op jit(solution)/shard_map/ppermute | solution.py:714
  88.2 26.5 %collective-permute-start.6 = (bf16[320,1024]{1,0:T(8,128)(2,1)S(1)}, bf16[320,1024]{1,0:T(8,128)(2,1)}, u32[]{:S(2)}, u32[]{:S(2)}) collective-permute-start(bf16[320,1024]{1,0:T(8,128)(2,1)S(1)} %maximum_select_fusion.2.refs_2_.refs_10_), channel_id=1, source_target_pairs={{0,2},{1,3},{2,0},{3,1},{4,6},{5,7},{6,4},{7,5},{8,10},{9,11},{10,... | collective-permute-start | bytes 1966088 | tf_op jit(solution)/shard_map/ppermute | solution.py:711
  106.2 21.0 %all-to-all-start.1 = ((bf16[4,64,640]{2,1,0:T(8,128)(2,1)}), bf16[4,64,640]{2,1,0:T(8,128)(2,1)}, u32[]{:S(2)}, u32[]{:S(2)}) async-start(bf16[4,64,640]{2,1,0:T(8,128)(2,1)} %get-tuple-element.127), calls=%async_computation.1 | async-start | bytes 655360 | tf_op jit(solution)/shard_map/all_to_all | solution.py:720
  114.1 21.9 %collective-permute-start.8 = (bf16[256,1024]{1,0:T(8,128)(2,1)}, bf16[256,1024]{1,0:T(8,128)(2,1)S(1)}, u32[]{:S(2)}, u32[]{:S(2)}) collective-permute-start(bf16[256,1024]{1,0:T(8,128)(2,1)} %pick.1.refs_3_), channel_id=1, source_target_pairs={{0,2},{1,3},{2,0},{3,1},{4,6},{5,7},{6,4},{7,5},{8,10},{9,11},{10,... | collective-permute-start | bytes 1572872 | tf_op jit(solution)/shard_map/ppermute | solution.py:711
  208.1 32.7 %collective-permute-start.20 = (bf16[1056,512]{1,0:T(8,128)(2,1)}, bf16[1056,512]{1,0:T(8,128)(2,1)}, u32[]{:S(2)}, u32[]{:S(2)}) collective-permute-start(bf16[1056,512]{1,0:T(8,128)(2,1)} %get-tuple-element.164), channel_id=1, source_target_pairs={{0,16},{16,0},{1,17},{17,1},{2,18},{18,2},{3,19},{19,3},{4,20},{20... | collective-permute-start | bytes 3244040 | tf_op jit(solution)/shard_map/ppermute | solution.py:714
  234.2 44.3 %collective-permute-start.23 = (bf16[1056,512]{1,0:T(8,128)(2,1)}, bf16[1056,512]{1,0:T(8,128)(2,1)}, u32[]{:S(2)}, u32[]{:S(2)}) collective-permute-start(bf16[1056,512]{1,0:T(8,128)(2,1)} %get-tuple-element.178), channel_id=1, source_target_pairs={{0,16},{16,0},{1,17},{17,1},{2,18},{18,2},{3,19},{19,3},{4,20},{20... | collective-permute-start | bytes 3244040 | tf_op jit(solution)/shard_map/ppermute | solution.py:714
  247.1 31.4 %collective-permute-start.22 = (bf16[1056,512]{1,0:T(8,128)(2,1)}, bf16[1056,512]{1,0:T(8,128)(2,1)}, u32[]{:S(2)}, u32[]{:S(2)}) collective-permute-start(bf16[1056,512]{1,0:T(8,128)(2,1)} %join.3.refs_0_), channel_id=1, source_target_pairs={{0,4},{12,8},{1,5},{13,9},{2,6},{14,10},{3,7},{15,11},{16,20},{28,... | collective-permute-start | bytes 3244040 | tf_op jit(solution)/shard_map/ppermute | solution.py:737
  249.8 72.7 %collective-permute-start.19 = (bf16[2,320,1024]{2,1,0:T(8,128)(2,1)}, bf16[2,320,1024]{2,1,0:T(8,128)(2,1)}, u32[]{:S(2)}, u32[]{:S(2)}) collective-permute-start(bf16[2,320,1024]{2,1,0:T(8,128)(2,1)} %get-tuple-element.162), channel_id=1, source_target_pairs={{0,1},{1,0},{2,3},{3,2},{4,5},{5,4},{6,7},{7,6},{8,9},{9,8},{10,11... | collective-permute-start | bytes 3932168 | tf_op jit(solution)/shard_map/ppermute | solution.py:708
  249.8 65.7 %collective-permute-start.24 = (bf16[320,1024]{1,0:T(8,128)(2,1)}, bf16[320,1024]{1,0:T(8,128)(2,1)}, u32[]{:S(2)}, u32[]{:S(2)}) collective-permute-start(bf16[320,1024]{1,0:T(8,128)(2,1)} %copy-done.16), channel_id=1, source_target_pairs={{0,2},{1,3},{2,0},{3,1},{4,6},{5,7},{6,4},{7,5},{8,10},{9,11},{10,... | collective-permute-start | bytes 1966088 | tf_op jit(solution)/shard_map/ppermute | solution.py:711
  311.1 51.3 %all-to-all-start.5 = ((bf16[4,384,640]{2,1,0:T(8,128)(2,1)}), bf16[4,384,640]{2,1,0:T(8,128)(2,1)}, u32[]{:S(2)}, u32[]{:S(2)}) async-start(bf16[4,384,640]{2,1,0:T(8,128)(2,1)} %attend_back.3), calls=%async_computation.5 | async-start | bytes 3932160 | tf_op jit(solution)/shard_map/all_to_all | solution.py:720
  324.7 46.6 %collective-permute-start.27 = (bf16[1056,512]{1,0:T(8,128)(2,1)}, bf16[1056,512]{1,0:T(8,128)(2,1)}, u32[]{:S(2)}, u32[]{:S(2)}) collective-permute-start(bf16[1056,512]{1,0:T(8,128)(2,1)} %get-tuple-element.180.refs_0_), channel_id=1, source_target_pairs={{4,8},{8,4},{5,9},{9,5},{6,10},{10,6},{7,11},{11,7},{20,24},{24,20... | collective-permute-start | bytes 3244040 | tf_op jit(solution)/shard_map/ppermute | solution.py:740
  326.3 45.0 %collective-permute-start.28 = (bf16[1056,512]{1,0:T(8,128)(2,1)}, bf16[1056,512]{1,0:T(8,128)(2,1)}, u32[]{:S(2)}, u32[]{:S(2)}) collective-permute-start(bf16[1056,512]{1,0:T(8,128)(2,1)} %get-tuple-element.197.refs_2_), channel_id=1, source_target_pairs={{0,4},{12,8},{1,5},{13,9},{2,6},{14,10},{3,7},{15,11},{16,20},{28,... | collective-permute-start | bytes 3244040 | tf_op jit(solution)/shard_map/ppermute | solution.py:737
  368.8 24.1 %collective-permute-start.29 = (bf16[2048,256]{1,0:T(8,128)(2,1)}, bf16[2048,256]{1,0:T(8,128)(2,1)}, u32[]{:S(2)}, u32[]{:S(2)}) collective-permute-start(bf16[2048,256]{1,0:T(8,128)(2,1)} %get-tuple-element.203), channel_id=1, source_target_pairs={{0,16},{16,0},{1,17},{17,1},{2,18},{18,2},{3,19},{19,3},{4,20},{20... | collective-permute-start | bytes 3145736 | tf_op jit(solution)/shard_map/ppermute | solution.py:714
  383.5 27.0 %collective-permute-start.34 = (bf16[320,1024]{1,0:T(8,128)(2,1)}, bf16[320,1024]{1,0:T(8,128)(2,1)}, u32[]{:S(2)}, u32[]{:S(2)}) collective-permute-start(bf16[320,1024]{1,0:T(8,128)(2,1)} %get-tuple-element.209), channel_id=1, source_target_pairs={{0,1},{1,0},{2,3},{3,2},{4,5},{5,4},{6,7},{7,6},{8,9},{9,8},{10,11... | collective-permute-start | bytes 1966088 | tf_op jit(solution)/shard_map/ppermute | solution.py:708
  383.6 30.9 %collective-permute-start.40 = (bf16[1056,512]{1,0:T(8,128)(2,1)}, bf16[1056,512]{1,0:T(8,128)(2,1)}, u32[]{:S(2)}, u32[]{:S(2)}) collective-permute-start(bf16[1056,512]{1,0:T(8,128)(2,1)} %get-tuple-element.216), channel_id=1, source_target_pairs={{4,8},{8,4},{5,9},{9,5},{6,10},{10,6},{7,11},{11,7},{20,24},{24,20... | collective-permute-start | bytes 3244040 | tf_op jit(solution)/shard_map/ppermute | solution.py:740
  397.2 34.1 %collective-permute-start.36 = (bf16[1056,512]{1,0:T(8,128)(2,1)}, bf16[1056,512]{1,0:T(8,128)(2,1)S(1)}, u32[]{:S(2)}, u32[]{:S(2)}) collective-permute-start(bf16[1056,512]{1,0:T(8,128)(2,1)} %get-tuple-element.200), channel_id=1, source_target_pairs={{4,0},{8,12},{5,1},{9,13},{6,2},{10,14},{7,3},{11,15},{20,16},{24,... | collective-permute-start | bytes 3244040 | tf_op jit(solution)/shard_map/ppermute | solution.py:743
  398.5 40.9 %collective-permute-start.37 = (bf16[320,1024]{1,0:T(8,128)(2,1)}, bf16[320,1024]{1,0:T(8,128)(2,1)S(1)}, u32[]{:S(2)}, u32[]{:S(2)}) collective-permute-start(bf16[320,1024]{1,0:T(8,128)(2,1)} %get-tuple-element.213), channel_id=1, source_target_pairs={{0,1},{1,0},{2,3},{3,2},{4,5},{5,4},{6,7},{7,6},{8,9},{9,8},{10,11... | collective-permute-start | bytes 1966088 | tf_op jit(solution)/shard_map/ppermute | solution.py:708
  400.6 32.2 %collective-permute-start.30 = (bf16[2048,256]{1,0:T(8,128)(2,1)}, bf16[2048,256]{1,0:T(8,128)(2,1)S(1)}, u32[]{:S(2)}, u32[]{:S(2)}) collective-permute-start(bf16[2048,256]{1,0:T(8,128)(2,1)} %add_convert_fusion.3), channel_id=1, source_target_pairs={{0,4},{12,8},{1,5},{13,9},{2,6},{14,10},{3,7},{15,11},{16,20},{28,... | collective-permute-start | bytes 3145736 | tf_op jit(solution)/shard_map/ppermute | solution.py:737
  416.2 37.7 %collective-permute-start.41 = (bf16[1056,512]{1,0:T(8,128)(2,1)S(1)}, bf16[1056,512]{1,0:T(8,128)(2,1)S(1)}, u32[]{:S(2)}, u32[]{:S(2)}) collective-permute-start(bf16[1056,512]{1,0:T(8,128)(2,1)S(1)} %add_convert_fusion), channel_id=1, source_target_pairs={{4,0},{8,12},{5,1},{9,13},{6,2},{10,14},{7,3},{11,15},{20,16},{24,... | collective-permute-start | bytes 3244040 | tf_op jit(solution)/shard_map/ppermute | solution.py:743
  433.3 20.6 %collective-permute-start.38 = (bf16[2048,256]{1,0:T(8,128)(2,1)S(1)}, bf16[2048,256]{1,0:T(8,128)(2,1)S(1)}, u32[]{:S(2)}, u32[]{:S(2)}) collective-permute-start(bf16[2048,256]{1,0:T(8,128)(2,1)S(1)} %add_convert_fusion.2), channel_id=1, source_target_pairs={{4,8},{8,4},{5,9},{9,5},{6,10},{10,6},{7,11},{11,7},{20,24},{24,20... | collective-permute-start | bytes 3145736 | tf_op jit(solution)/shard_map/ppermute | solution.py:740
  454.4 29.8 %collective-permute-start.42 = (bf16[2048,256]{1,0:T(8,128)(2,1)S(1)}, bf16[2048,256]{1,0:T(8,128)(2,1)S(1)}, u32[]{:S(2)}, u32[]{:S(2)}) collective-permute-start(bf16[2048,256]{1,0:T(8,128)(2,1)S(1)} %add_convert_fusion.1), channel_id=1, source_target_pairs={{4,0},{8,12},{5,1},{9,13},{6,2},{10,14},{7,3},{11,15},{20,16},{24,... | collective-permute-start | bytes 3145736 | tf_op jit(solution)/shard_map/ppermute | solution.py:743
  (58 other events, 553.1 us)
